TPU v7x, 32 devices: a whole 2x2x4 slice. The times are simulated.
32 devices in a mesh: section: 2 (over x), shard: 4 (over y, core), replica: 4 (over z).
Axes of the slice: x: 2, y: 2, z: 4, core: 2. Of those that a mesh axis runs over, the one named last changes fastest.
Arguments:
- block_input: bfloat16 [2, 16, 218, 1536], P(None, ('shard', 'replica')), may hold values from -6 to 6
- modulation: float32 [2, 2, 16, 2, 6, 1536], P('section', None, ('shard', 'replica')), may hold values from -4 to 4
- w_qkv: bfloat16 [2, 2, 1536, 4608], P('section', None, 'shard'), may hold values from -0.15625 to 0.15625
- b_qkv: bfloat16 [2, 2, 4608], P('section', None, 'shard'), may hold values from -3 to 3
- qk_gain: bfloat16 [2, 2, 2, 64], P('section', None, None, 'shard'), may hold values from 0.099609375 to 1.8984375
- w_out: bfloat16 [2, 2, 1536, 1536], P('section', None, 'shard'), may hold values from -1.25 to 1.25
- b_out: bfloat16 [2, 2, 1536], P('section', None, 'shard'), may hold values from -3 to 3
- w_fc1: bfloat16 [2, 2, 1536, 6144], P('section', None, 'shard'), may hold values from -0.15625 to 0.15625
- b_fc1: bfloat16 [2, 2, 6144], P('section', None, 'shard'), may hold values from -3 to 3
- w_fc2: bfloat16 [2, 2, 6144, 1536], P('section', None, 'shard'), may hold values from -0.078125 to 0.078125
- b_fc2: bfloat16 [2, 2, 1536], P('section', None, 'shard'), may hold values from -3 to 3
- cotangent: bfloat16 [2, 16, 218, 1536], P(None, ('shard', 'replica')), may hold values from -6 to 6
Outputs:
- activations: bfloat16 [2, 2, 16, 218, 1536], P('section', None, ('shard', 'replica'))
- input_grads: float32 [2, 2, 16, 218, 1536], P('section', None, ('shard', 'replica'))
- modulation_grad: float32 [2, 2, 16, 2, 6, 1536], P('section', None, ('shard', 'replica'))
- w_qkv_grad: float32 [2, 2, 1536, 4608], P('section', None, ('shard', 'replica'))
- b_qkv_grad: float32 [2, 2, 4608], P('section', None, ('shard', 'replica'))
- qk_gain_grad: float32 [2, 2, 2, 64], P('section', None, None, ('shard', 'replica'))
- w_out_grad: float32 [2, 2, 1536, 1536], P('section', None, ('shard', 'replica'))
- b_out_grad: float32 [2, 2, 1536], P('section', None, ('shard', 'replica'))
- w_fc1_grad: float32 [2, 2, 1536, 6144], P('section', None, ('shard', 'replica'))
- b_fc1_grad: float32 [2, 2, 6144], P('section', None, ('shard', 'replica'))
- w_fc2_grad: float32 [2, 2, 6144, 1536], P('section', None, ('shard', 'replica'))
- b_fc2_grad: float32 [2, 2, 1536], P('section', None, ('shard', 'replica'))
All inputs are finite; a program needn't handle non-finite values.
Results may differ from a plain program's by a relative error of at most 0.017.
Values may be sent and summed in bfloat16 or wider, within the bound.
No kernel may reach another device: no remote copies, remote signals or barrier semaphores. Data moves between devices by JAX's collectives and lax.ppermute only.
A program may use at most 704 MiB of HBM per device.

v0:
```python
import jax
import jax.numpy as jnp
from jax import lax
from jax.sharding import PartitionSpec as P

IMG = 64


norm_eps = 1e-06


def from_behind(x, axis, by):
    count = lax.axis_size(axis)
    pairs = [(i, i + by) for i in range(count) if 0 <= i + by < count]
    return lax.ppermute(x, axis, pairs)


def layer_norm_mod(segment, shift_row, scale_row):
    centred = segment - jnp.mean(segment, -1, keepdims=True)
    normed = centred * lax.rsqrt(jnp.mean(centred * centred, -1, keepdims=True) + norm_eps)
    return normed * (1.0 + scale_row) + shift_row


def head_norm(values, head_gain):
    return values * lax.rsqrt(jnp.mean(values * values, -1, keepdims=True) + norm_eps) * head_gain


def pair_norm(pair_rows, pair_gain):
    return head_norm(pair_rows, pair_gain[:, None, :])


def tanh_gelu_activation(values):
    return jax.nn.gelu(values, approximate=True)


def forward_pass(section_in, modulation_mb, weights):
    projection_weight, b_proj, gain_set, backward_weight, b_back, w_up, b_up, w_down, b_down = (
        weights
    )
    seq_count, length, model_width = section_in.shape
    head_dim = gain_set.shape[-1]
    head_count = model_width // head_dim
    scale_qk = head_dim ** (-0.5)
    stream_bounds = ((0, IMG), (IMG, length))
    section_rows = section_in.astype(jnp.float32)
    hidden_list, pair_list, query_list, key_list, value_list = ([], [], [], [], [])
    for token_stream in range(2):
        row_start, row_stop = stream_bounds[token_stream]
        segment = section_rows[:, row_start:row_stop]
        hidden_state = layer_norm_mod(
            segment,
            modulation_mb[:, token_stream, 0][:, None],
            modulation_mb[:, token_stream, 1][:, None],
        ).astype(jnp.bfloat16)
        projected = jnp.einsum(
            "lyv,vi->lyi",
            hidden_state,
            projection_weight[token_stream],
            preferred_element_type=jnp.float32,
        )
        projected = projected + b_proj[token_stream].astype(jnp.float32)
        shaped = projected.reshape(seq_count, row_stop - row_start, 3, head_count, head_dim)
        pair_rows = shaped[:, :, :2]
        normed_pair = pair_norm(pair_rows, gain_set[token_stream].astype(jnp.float32)).astype(
            jnp.bfloat16
        )
        hidden_list.append(hidden_state)
        pair_list.append(pair_rows)
        query_list.append(normed_pair[:, :, 0])
        key_list.append(normed_pair[:, :, 1])
        value_list.append(shaped[:, :, 2].astype(jnp.bfloat16))
    query_all = jnp.concatenate(query_list, 1)
    key_all = jnp.concatenate(key_list, 1)
    value_all = jnp.concatenate(value_list, 1)
    scores = (
        jnp.einsum("sqhd,skhd->shqk", query_all, key_all, preferred_element_type=jnp.float32)
        * scale_qk
    )
    exponent = jnp.exp(scores)
    denominator = jnp.sum(exponent, -1, keepdims=True)
    soft_weights = (exponent / denominator).astype(jnp.bfloat16)
    attended = jnp.einsum(
        "shqk,skhd->sqhd", soft_weights, value_all, preferred_element_type=jnp.float32
    )
    attended = attended.astype(jnp.bfloat16).reshape(seq_count, length, model_width)
    mixed_list, branch_list = ([], [])
    for token_stream in range(2):
        row_start, row_stop = stream_bounds[token_stream]
        branch = jnp.einsum(
            "lyv,vi->lyi",
            attended[:, row_start:row_stop],
            backward_weight[token_stream],
            preferred_element_type=jnp.float32,
        ) + b_back[token_stream].astype(jnp.float32)
        mixed_list.append(
            section_rows[:, row_start:row_stop]
            + modulation_mb[:, token_stream, 2][:, None] * branch
        )
        branch_list.append(branch)
    mixed = jnp.concatenate(mixed_list, 1)
    final_list, hidden_mlp_list, pre_list, activated_list, mlp_out_list = ([], [], [], [], [])
    for token_stream in range(2):
        row_start, row_stop = stream_bounds[token_stream]
        segment = mixed[:, row_start:row_stop]
        hidden_mlp = layer_norm_mod(
            segment,
            modulation_mb[:, token_stream, 3][:, None],
            modulation_mb[:, token_stream, 4][:, None],
        ).astype(jnp.bfloat16)
        pre_act = jnp.einsum(
            "snd,df->snf", hidden_mlp, w_up[token_stream], preferred_element_type=jnp.float32
        )
        pre_act = pre_act + b_up[token_stream].astype(jnp.float32)
        activated = tanh_gelu_activation(pre_act).astype(jnp.bfloat16)
        mlp_out = jnp.einsum(
            "snf,fd->snd", activated, w_down[token_stream], preferred_element_type=jnp.float32
        )
        mlp_out = mlp_out + b_down[token_stream].astype(jnp.float32)
        final_list.append(segment + modulation_mb[:, token_stream, 5][:, None] * mlp_out)
        hidden_mlp_list.append(hidden_mlp)
        pre_list.append(pre_act)
        activated_list.append(activated)
        mlp_out_list.append(mlp_out)
    kept_state = (
        section_in,
        jnp.concatenate(hidden_list, 1),
        jnp.concatenate(pair_list, 1),
        query_all,
        key_all,
        value_all,
        jnp.log(denominator),
        attended,
        jnp.concatenate(branch_list, 1),
        mixed,
        jnp.concatenate(hidden_mlp_list, 1),
        jnp.concatenate(pre_list, 1),
        jnp.concatenate(activated_list, 1),
        jnp.concatenate(mlp_out_list, 1),
    )
    return (jnp.concatenate(final_list, 1), kept_state)


def backward_pass(grad_out, modulation_mb, weights, kept_state):
    projection_weight, b_proj, gain_set, backward_weight, b_back, w_up, b_up, w_down, b_down = (
        weights
    )
    (
        section_in,
        hidden_all,
        pair_all,
        query_all,
        key_all,
        value_all,
        log_total,
        attended,
        branch_all,
        mixed,
        hidden_mlp_all,
        pre_all,
        activated_all,
        mlp_out_all,
    ) = kept_state
    seq_count, length, model_width = section_in.shape
    head_dim = gain_set.shape[-1]
    head_count = model_width // head_dim
    scale_qk = head_dim ** (-0.5)
    stream_bounds = ((0, IMG), (IMG, length))
    section_rows = section_in.astype(jnp.float32)
    mixed_grad_list, late_list, mlp_grad_list, pre_grad_list, bup_list, bdown_list = (
        [],
        [],
        [],
        [],
        [],
        [],
    )
    for token_stream in range(2):
        row_start, row_stop = stream_bounds[token_stream]
        upstream = grad_out[:, row_start:row_stop]
        mlp_grad = (modulation_mb[:, token_stream, 5][:, None] * upstream).astype(jnp.bfloat16)
        gate_late = jnp.sum(mlp_out_all[:, row_start:row_stop] * upstream, 1)
        activated_grad = jnp.einsum(
            "snd,fd->snf", mlp_grad, w_down[token_stream], preferred_element_type=jnp.float32
        )
        _, gelu_pull = jax.vjp(tanh_gelu_activation, pre_all[:, row_start:row_stop])
        pre_grad = gelu_pull(activated_grad)[0].astype(jnp.bfloat16)
        hidden_mlp_grad = jnp.einsum(
            "snf,df->snd", pre_grad, w_up[token_stream], preferred_element_type=jnp.float32
        )
        _, late_pull = jax.vjp(
            layer_norm_mod,
            mixed[:, row_start:row_stop],
            modulation_mb[:, token_stream, 3][:, None],
            modulation_mb[:, token_stream, 4][:, None],
        )
        segment_grad, shift_grad, scale_grad = late_pull(hidden_mlp_grad)
        mixed_grad_list.append(upstream + segment_grad)
        late_list.append((shift_grad[:, 0], scale_grad[:, 0], gate_late))
        mlp_grad_list.append(mlp_grad)
        pre_grad_list.append(pre_grad)
        bup_list.append(jnp.sum(pre_grad.astype(jnp.float32), (0, 1)))
        bdown_list.append(jnp.sum(mlp_grad.astype(jnp.float32), (0, 1)))
    mixed_grad = jnp.concatenate(mixed_grad_list, 1)
    back_list, gate_list, branch_grad_list, bback_list = ([], [], [], [])
    for token_stream in range(2):
        row_start, row_stop = stream_bounds[token_stream]
        mixed_part = mixed_grad[:, row_start:row_stop]
        branch_gradient = (modulation_mb[:, token_stream, 2][:, None] * mixed_part).astype(
            jnp.bfloat16
        )
        gate_list.append(jnp.sum(branch_all[:, row_start:row_stop] * mixed_part, 1))
        branch_grad_list.append(branch_gradient)
        bback_list.append(jnp.sum(branch_gradient.astype(jnp.float32), (0, 1)))
        back_list.append(
            jnp.einsum(
                "mqb,hb->mqh",
                branch_gradient,
                backward_weight[token_stream],
                preferred_element_type=jnp.float32,
            )
        )
    attended_grad = jnp.concatenate(back_list, 1).astype(jnp.bfloat16)
    attended_grad = attended_grad.reshape(seq_count, length, head_count, head_dim)
    scores = (
        jnp.einsum("sqhd,skhd->shqk", query_all, key_all, preferred_element_type=jnp.float32)
        * scale_qk
    )
    soft_exact = jnp.exp(scores - log_total)
    soft_low = soft_exact.astype(jnp.bfloat16)
    value_grad = jnp.einsum(
        "shqk,sqhd->skhd", soft_low, attended_grad, preferred_element_type=jnp.float32
    )
    prob_grad = jnp.einsum(
        "sqhd,skhd->shqk", attended_grad, value_all, preferred_element_type=jnp.float32
    )
    row_delta = jnp.sum(prob_grad * soft_exact, -1, keepdims=True)
    score_grad = (soft_exact * (prob_grad - row_delta)).astype(jnp.bfloat16)
    query_grad = (
        jnp.einsum("shqk,skhd->sqhd", score_grad, key_all, preferred_element_type=jnp.float32)
        * scale_qk
    )
    key_grad = (
        jnp.einsum("shqk,sqhd->skhd", score_grad, query_all, preferred_element_type=jnp.float32)
        * scale_qk
    )
    proj_grad_list, proj_b_list, gain_list, input_list, modul_list = ([], [], [], [], [])
    for token_stream in range(2):
        row_start, row_stop = stream_bounds[token_stream]
        row_total = row_stop - row_start
        pair_grad = jnp.stack(
            [query_grad[:, row_start:row_stop], key_grad[:, row_start:row_stop]], 2
        )
        _, pair_pull = jax.vjp(
            pair_norm, pair_all[:, row_start:row_stop], gain_set[token_stream].astype(jnp.float32)
        )
        pair_rows_grad, gain_grad = pair_pull(pair_grad)
        projected_gradient = jnp.concatenate(
            [pair_rows_grad, value_grad[:, row_start:row_stop, None]], 2
        )
        projected_gradient = projected_gradient.reshape(
            seq_count, row_total, 3 * model_width
        ).astype(jnp.bfloat16)
        proj_grad_list.append(projected_gradient)
        proj_b_list.append(jnp.sum(projected_gradient.astype(jnp.float32), (0, 1)))
        gain_list.append(gain_grad)
        hidden_grad = jnp.einsum(
            "mqb,hb->mqh",
            projected_gradient,
            projection_weight[token_stream],
            preferred_element_type=jnp.float32,
        )
        _, norm_backward_map = jax.vjp(
            layer_norm_mod,
            section_rows[:, row_start:row_stop],
            modulation_mb[:, token_stream, 0][:, None],
            modulation_mb[:, token_stream, 1][:, None],
        )
        segment_grad, shift_grad, scale_grad = norm_backward_map(hidden_grad)
        input_list.append(mixed_grad[:, row_start:row_stop] + segment_grad)
        late_shift, late_scale, late_gate = late_list[token_stream]
        modul_list.append(
            jnp.stack(
                [
                    shift_grad[:, 0],
                    scale_grad[:, 0],
                    gate_list[token_stream],
                    late_shift,
                    late_scale,
                    late_gate,
                ],
                1,
            )
        )
    small_terms = (
        jnp.stack(proj_b_list),
        jnp.stack(gain_list),
        jnp.stack(bback_list),
        jnp.stack(bup_list),
        jnp.stack(bdown_list),
    )
    matrix_ops = (
        (hidden_all, jnp.concatenate(proj_grad_list, 1)),
        (attended, jnp.concatenate(branch_grad_list, 1)),
        (hidden_mlp_all, jnp.concatenate(pre_grad_list, 1)),
        (activated_all, jnp.concatenate(mlp_grad_list, 1)),
    )
    return (jnp.concatenate(input_list, 1), jnp.stack(modul_list, 1), small_terms, matrix_ops)


def matrix_terms(left, right):
    image_part = jnp.einsum(
        "xnd,xne->de", left[:, :IMG], right[:, :IMG], preferred_element_type=jnp.float32
    )
    text_part = jnp.einsum(
        "xnd,xne->de", left[:, IMG:], right[:, IMG:], preferred_element_type=jnp.float32
    )
    return jnp.stack([image_part, text_part], 1)


def reduce_matrix(left, right):
    group_sum = lax.psum_scatter(
        matrix_terms(left, right).astype(jnp.bfloat16), "shard", scatter_dimension=0, tiled=True
    )
    summed = lax.psum_scatter(group_sum, "replica", scatter_dimension=0, tiled=True).astype(
        jnp.float32
    )
    return jnp.swapaxes(summed, 0, 1)[None]


def per_device(
    block_input,
    modulation,
    w_qkv,
    b_qkv,
    qk_gain,
    w_out,
    b_out,
    w_fc1,
    b_fc1,
    w_fc2,
    b_fc2,
    cotangent,
):
    section_id = lax.axis_index("section")
    micro_count = block_input.shape[0]
    modul_all = modulation[0]
    own_shards = (
        w_qkv[0],
        b_qkv[0],
        qk_gain[0],
        w_out[0],
        b_out[0],
        w_fc1[0],
        b_fc1[0],
        w_fc2[0],
        b_fc2[0],
    )
    weights = (
        lax.all_gather(own_shards[0], "shard", axis=1, tiled=True),
        lax.all_gather(own_shards[1], "shard", axis=1, tiled=True),
        lax.all_gather(own_shards[2], "shard", axis=2, tiled=True),
        lax.all_gather(own_shards[3], "shard", axis=1, tiled=True),
        lax.all_gather(own_shards[4], "shard", axis=1, tiled=True),
        lax.all_gather(own_shards[5], "shard", axis=1, tiled=True),
        lax.all_gather(own_shards[6], "shard", axis=1, tiled=True),
        lax.all_gather(own_shards[7], "shard", axis=1, tiled=True),
        lax.all_gather(own_shards[8], "shard", axis=1, tiled=True),
    )
    received = jnp.zeros(block_input.shape[1:], jnp.bfloat16)
    activations = jnp.zeros(block_input.shape, jnp.bfloat16)
    kept_list = []
    for clock_tick in range(micro_count + 1):
        mb_index = clock_tick - section_id
        is_valid = (mb_index >= 0) & (mb_index < micro_count)
        mb_slot = jnp.clip(mb_index, 0, micro_count - 1)
        own_input = block_input[min(clock_tick, micro_count - 1)]
        section_in = jnp.where(section_id == 0, own_input, received)
        modulation_mb = lax.dynamic_index_in_dim(modul_all, mb_slot, 0, keepdims=False)
        result, kept_state = forward_pass(section_in, modulation_mb, weights)
        sent_rows = result.astype(jnp.bfloat16)
        activations = jnp.where(
            is_valid,
            lax.dynamic_update_index_in_dim(activations, sent_rows, mb_slot, 0),
            activations,
        )
        kept_list.append(kept_state)
        if clock_tick < micro_count:
            received = from_behind(sent_rows, "section", 1)
    back_weights = (
        lax.all_gather(own_shards[0], "shard", axis=1, tiled=True),
        lax.all_gather(own_shards[1], "shard", axis=1, tiled=True),
        lax.all_gather(own_shards[2], "shard", axis=2, tiled=True),
        lax.all_gather(own_shards[3], "shard", axis=1, tiled=True),
        lax.all_gather(own_shards[4], "shard", axis=1, tiled=True),
        lax.all_gather(own_shards[5], "shard", axis=1, tiled=True),
        lax.all_gather(own_shards[6], "shard", axis=1, tiled=True),
        lax.all_gather(own_shards[7], "shard", axis=1, tiled=True),
        lax.all_gather(own_shards[8], "shard", axis=1, tiled=True),
    )
    stacked = jax.tree.map(lambda *members: jnp.stack(members), *kept_list)
    grads_in = jnp.zeros(cotangent.shape[1:], jnp.bfloat16)
    input_grads = jnp.zeros(cotangent.shape, jnp.float32)
    modulation_grad = jnp.zeros(modul_all.shape, jnp.float32)
    small_totals = None
    ops_list = []
    for clock_tick in range(micro_count + 1):
        mb_index = clock_tick - 1 + section_id
        is_valid = (mb_index >= 0) & (mb_index < micro_count)
        mb_slot = jnp.clip(mb_index, 0, micro_count - 1)
        fwd_tick = jnp.clip(clock_tick - 1 + 2 * section_id, 0, micro_count)
        kept_state = jax.tree.map(
            lambda member: lax.dynamic_index_in_dim(member, fwd_tick, 0, keepdims=False), stacked
        )
        last_grad = lax.dynamic_index_in_dim(cotangent, mb_slot, 0, keepdims=False)
        upstream = jnp.where(section_id == 1, last_grad, grads_in).astype(jnp.float32)
        upstream = jnp.where(is_valid, upstream, 0.0)
        modulation_mb = lax.dynamic_index_in_dim(modul_all, mb_slot, 0, keepdims=False)
        input_grad, modul_grad, small_terms, matrix_ops = backward_pass(
            upstream, modulation_mb, back_weights, kept_state
        )
        small_totals = (
            small_terms
            if small_totals is None
            else jax.tree.map(jnp.add, small_totals, small_terms)
        )
        ops_list.append(matrix_ops)
        input_grads = jnp.where(
            is_valid,
            lax.dynamic_update_index_in_dim(input_grads, input_grad, mb_slot, 0),
            input_grads,
        )
        modulation_grad = jnp.where(
            is_valid,
            lax.dynamic_update_index_in_dim(modulation_grad, modul_grad, mb_slot, 0),
            modulation_grad,
        )
        if clock_tick < micro_count:
            grads_in = from_behind(input_grad.astype(jnp.bfloat16), "section", -1)
    first_valid = 1 - section_id
    matrix_grads = []
    for matrix_id in range(4):
        left_all = jnp.stack([ops[matrix_id][0] for ops in ops_list], 0)
        right_all = jnp.stack([ops[matrix_id][1] for ops in ops_list], 0)
        left = lax.dynamic_slice_in_dim(left_all, first_valid, micro_count, 0)
        right = lax.dynamic_slice_in_dim(right_all, first_valid, micro_count, 0)
        left = left.reshape((-1,) + left.shape[2:])
        right = right.reshape((-1,) + right.shape[2:])
        matrix_grads.append(reduce_matrix(left, right))
    group_small = (
        lax.psum_scatter(
            small_totals[0].astype(jnp.bfloat16), "shard", scatter_dimension=1, tiled=True
        ).astype(jnp.float32),
        lax.psum_scatter(
            small_totals[1].astype(jnp.bfloat16), "shard", scatter_dimension=2, tiled=True
        ).astype(jnp.float32),
        lax.psum_scatter(
            small_totals[2].astype(jnp.bfloat16), "shard", scatter_dimension=1, tiled=True
        ).astype(jnp.float32),
        lax.psum_scatter(
            small_totals[3].astype(jnp.bfloat16), "shard", scatter_dimension=1, tiled=True
        ).astype(jnp.float32),
        lax.psum_scatter(
            small_totals[4].astype(jnp.bfloat16), "shard", scatter_dimension=1, tiled=True
        ).astype(jnp.float32),
    )
    small_sums = (
        lax.psum_scatter(group_small[0], "replica", scatter_dimension=1, tiled=True),
        lax.psum_scatter(group_small[1], "replica", scatter_dimension=2, tiled=True),
        lax.psum_scatter(group_small[2], "replica", scatter_dimension=1, tiled=True),
        lax.psum_scatter(group_small[3], "replica", scatter_dimension=1, tiled=True),
        lax.psum_scatter(group_small[4], "replica", scatter_dimension=1, tiled=True),
    )
    return (
        activations[None],
        input_grads[None],
        modulation_grad[None],
        matrix_grads[0],
        small_sums[0][None],
        small_sums[1][None],
        matrix_grads[1],
        small_sums[2][None],
        matrix_grads[2],
        small_sums[3][None],
        matrix_grads[3],
        small_sums[4][None],
    )


def solution(mesh):
    return jax.shard_map(
        per_device,
        mesh=mesh,
        in_specs=(
            P(None, ("shard", "replica"), None, None),
            P("section", None, ("shard", "replica"), None, None, None),
            P("section", None, "shard", None),
            P("section", None, "shard"),
            P("section", None, None, "shard"),
            P("section", None, "shard", None),
            P("section", None, "shard"),
            P("section", None, "shard", None),
            P("section", None, "shard"),
            P("section", None, "shard", None),
            P("section", None, "shard"),
            P(None, ("shard", "replica"), None, None),
        ),
        out_specs=(
            P("section", None, ("shard", "replica"), None, None),
            P("section", None, ("shard", "replica"), None, None),
            P("section", None, ("shard", "replica"), None, None, None),
            P("section", None, ("shard", "replica"), None),
            P("section", None, ("shard", "replica")),
            P("section", None, None, ("shard", "replica")),
            P("section", None, ("shard", "replica"), None),
            P("section", None, ("shard", "replica")),
            P("section", None, ("shard", "replica"), None),
            P("section", None, ("shard", "replica")),
            P("section", None, ("shard", "replica"), None),
            P("section", None, ("shard", "replica")),
        ),
        check_vma=False,
    )
```

profile of v0, /device:TPU:0, one launch (start us, length us, event | category | flops | bytes accessed | tf_op | source)
XLA Modules:
  0.0 2880.1 jit_solution(1023249339588903521)
XLA Ops:
  57.2 19.6 all-gather.16.cloned.1.call-done
  84.9 165.2 %all-gather.14.cloned.1.call-done = bf16[1,2,1536,4608]{3,2,1,0:T(8,128)(2,1)} async-done(((bf16[1,2,384,4608]{3,2,1,0:T(8,128)(2,1)}), bf16[1,2,1536,4608]{3,2,1,0:T(8,128)(2,1)}) %all-gather.14.cloned.1.call-update) | async-done | bytes 28311568 | tf_op jit(solution)/shard_map/all_gather | solution.py:359
  261.9 13.4 convolution_add_fusion.2
  304.4 175.2 %all-gather.18.cloned.1.call-done = bf16[1,2,1536,6144]{3,2,1,0:T(8,128)(2,1)} async-done(((bf16[1,2,384,6144]{3,2,1,0:T(8,128)(2,1)}), bf16[1,2,1536,6144]{3,2,1,0:T(8,128)(2,1)}) %all-gather.18.cloned.1.call-update) | async-done | bytes 37748752 | tf_op jit(solution)/shard_map/all_gather | solution.py:364
  489.5 17.0 fusion.33
  506.5 202.4 %all-gather.20.cloned.1.call-done = bf16[1,2,6144,1536]{3,2,1,0:T(8,128)(2,1)} async-done(((bf16[1,2,1536,1536]{3,2,1,0:T(8,128)(2,1)}), bf16[1,2,6144,1536]{3,2,1,0:T(8,128)(2,1)}) %all-gather.20.cloned.1.call-update) | async-done | bytes 37748752 | tf_op jit(solution)/shard_map/all_gather | solution.py:366
  962.8 13.1 convert_reduce_fusion.11
  975.9 13.9 fusion.363
  1145.7 13.1 fusion.361
  1292.9 12.8 convert_reduce_fusion.9
  1430.5 19.6 pad_maximum_fusion.2
  1470.0 13.2 fusion.1
  1483.2 26.1 pad_maximum_fusion
  1543.6 17.6 fusion.3
  1561.2 28.3 pad_maximum_fusion.1
  1600.2 133.8 %reduce-scatter.37.cloned.1.call-done = bf16[384,2,4608]{2,0,1:T(8,128)(2,1)} async-done(((bf16[1536,2,4608]{2,0,1:T(8,128)(2,1)}), bf16[384,2,4608]{2,0,1:T(8,128)(2,1)}) %reduce-scatter.37.cloned.1.call-update) | async-done | bytes 7077904 | tf_op jit(solution)/shard_map/reduce_scatter | solution.py:321
  1734.0 260.2 %reduce-scatter.45.cloned.1.call-done = bf16[384,2,6144]{2,0,1:T(8,128)(2,1)} async-done(((bf16[1536,2,6144]{2,0,1:T(8,128)(2,1)}), bf16[384,2,6144]{2,0,1:T(8,128)(2,1)}) %reduce-scatter.45.cloned.1.call-update) | async-done | bytes 9437200 | tf_op jit(solution)/shard_map/reduce_scatter | solution.py:321
  1999.9 254.4 %reduce-scatter.49.cloned.1.call-done = bf16[1536,2,1536]{2,0,1:T(8,128)(2,1)} async-done(((bf16[6144,2,1536]{2,0,1:T(8,128)(2,1)}), bf16[1536,2,1536]{2,0,1:T(8,128)(2,1)}) %reduce-scatter.49.cloned.1.call-update) | async-done | bytes 9437200 | tf_op jit(solution)/shard_map/reduce_scatter | solution.py:321
  2327.0 14.1 reduce-scatter.55.cloned.1.call-done
  2342.7 22.6 reduce-scatter.65.cloned.1.call-done
  2366.9 47.8 %reduce-scatter.43.cloned.1.call-done = bf16[96,2,1536]{2,0,1:T(8,128)(2,1)} async-done(((bf16[384,2,1536]{2,0,1:T(8,128)(2,1)}), bf16[96,2,1536]{2,0,1:T(8,128)(2,1)}) %reduce-scatter.43.cloned.1.call-update) | async-done | bytes 589840 | tf_op jit(solution)/shard_map/reduce_scatter | solution.py:324
  2417.0 123.0 %reduce-scatter.39.cloned.1.call-done = bf16[96,2,4608]{2,0,1:T(8,128)(2,1)} async-done(((bf16[384,2,4608]{2,0,1:T(8,128)(2,1)}), bf16[96,2,4608]{2,0,1:T(8,128)(2,1)}) %reduce-scatter.39.cloned.1.call-update) | async-done | bytes 1769488 | tf_op jit(solution)/shard_map/reduce_scatter | solution.py:324
  2543.7 160.2 %reduce-scatter.47.cloned.1.call-done = bf16[96,2,6144]{2,0,1:T(8,128)(2,1)} async-done(((bf16[384,2,6144]{2,0,1:T(8,128)(2,1)}), bf16[96,2,6144]{2,0,1:T(8,128)(2,1)}) %reduce-scatter.47.cloned.1.call-update) | async-done | bytes 2359312 | tf_op jit(solution)/shard_map/reduce_scatter | solution.py:324
  2708.3 160.2 %reduce-scatter.51.cloned.1.call-done = bf16[384,2,1536]{2,0,1:T(8,128)(2,1)} async-done(((bf16[1536,2,1536]{2,0,1:T(8,128)(2,1)}), bf16[384,2,1536]{2,0,1:T(8,128)(2,1)}) %reduce-scatter.51.cloned.1.call-update) | async-done | bytes 2359312 | tf_op jit(solution)/shard_map/reduce_scatter | solution.py:324
  (1494 shorter events, 932.0 us)
Async XLA Ops:
  7.2 69.6 %all-gather.16.cloned.1.call-start = ((), (), s32[]{:S(2)}) async-start(), calls=%async_computation.26 | async-start | bytes 11796480 | tf_op jit(solution)/shard_map/all_gather | solution.py:362
  7.9 242.2 %all-gather.14.cloned.1.call-start = ((), (), s32[]{:S(2)}) async-start(), calls=%async_computation.25 | async-start | bytes 35389440 | tf_op jit(solution)/shard_map/all_gather | solution.py:359
  8.7 470.9 %all-gather.18.cloned.1.call-start = ((), (), s32[]{:S(2)}) async-start(), calls=%async_computation.27 | async-start | bytes 47185920 | tf_op jit(solution)/shard_map/all_gather | solution.py:364
  9.4 699.5 %all-gather.20.cloned.1.call-start = ((), (), s32[]{:S(2)}) async-start(), calls=%async_computation.28 | async-start | bytes 47185920 | tf_op jit(solution)/shard_map/all_gather | solution.py:366
  10.0 1581.1 %reduce-scatter.67.cloned.1.call-start = ((), (), s32[]{:S(2)}) async-start(), calls=%async_computation.36 | async-start | bytes 491520
  726.8 18.6 collective-permute-start
  837.6 18.8 collective-permute-start.1
  1110.7 18.3 collective-permute-start.2
  1345.4 247.7 %reduce-scatter.59.cloned.1.call-start = ((), (), s32[]{:S(2)}) async-start(), calls=%async_computation.32 | async-start | bytes 491520
  1361.1 233.9 %reduce-scatter.53.cloned.1.call-start = ((), (), s32[]{:S(2)}) async-start(), calls=%async_computation.29 | async-start | bytes 1474560
  1366.9 230.4 %reduce-scatter.63.cloned.1.call-start = ((), (), s32[]{:S(2)}) async-start(), calls=%async_computation.34 | async-start | bytes 1966080
  1380.2 219.5 %reduce-scatter.41.cloned.1.call-start = ((), (), s32[]{:S(2)}) async-start(), calls=%async_computation.19 | async-start | bytes 11796480 | tf_op jit(solution)/shard_map/reduce_scatter | solution.py:321
  1388.6 345.4 %reduce-scatter.37.cloned.1.call-start = ((), (), s32[]{:S(2)}) async-start(), calls=%async_computation.17 | async-start | bytes 35389440 | tf_op jit(solution)/shard_map/reduce_scatter | solution.py:321
  1450.2 544.0 %reduce-scatter.45.cloned.1.call-start = ((), (), s32[]{:S(2)}) async-start(), calls=%async_computation.21 | async-start | bytes 47185920 | tf_op jit(solution)/shard_map/reduce_scatter | solution.py:321
  1509.3 745.0 %reduce-scatter.49.cloned.1.call-start = ((), (), s32[]{:S(2)}) async-start(), calls=%async_computation.23 | async-start | bytes 47185920 | tf_op jit(solution)/shard_map/reduce_scatter | solution.py:321
  1589.6 721.3 %reduce-scatter.57.cloned.1.call-start = ((), (), s32[]{:S(2)}) async-start(), calls=%async_computation.31 | async-start | bytes 20480
  1591.1 733.0 %reduce-scatter.69.cloned.1.call-start = ((), (), s32[]{:S(2)}) async-start(), calls=%async_computation.37 | async-start | bytes 245760
  1593.0 732.5 %reduce-scatter.61.cloned.1.call-start = ((), (), s32[]{:S(2)}) async-start(), calls=%async_computation.33 | async-start | bytes 245760
  1595.0 746.2 %reduce-scatter.55.cloned.1.call-start = ((), (), s32[]{:S(2)}) async-start(), calls=%async_computation.30 | async-start | bytes 737280
  1597.2 768.1 %reduce-scatter.65.cloned.1.call-start = ((), (), s32[]{:S(2)}) async-start(), calls=%async_computation.35 | async-start | bytes 983040
  1599.6 815.2 %reduce-scatter.43.cloned.1.call-start = ((), (), s32[]{:S(2)}) async-start(), calls=%async_computation.20 | async-start | bytes 2949120 | tf_op jit(solution)/shard_map/reduce_scatter | solution.py:324
  1600.2 939.8 %reduce-scatter.39.cloned.1.call-start = ((), (), s32[]{:S(2)}) async-start(), calls=%async_computation.18 | async-start | bytes 8847360 | tf_op jit(solution)/shard_map/reduce_scatter | solution.py:324
  1734.0 969.9 %reduce-scatter.47.cloned.1.call-start = ((), (), s32[]{:S(2)}) async-start(), calls=%async_computation.22 | async-start | bytes 11796480 | tf_op jit(solution)/shard_map/reduce_scatter | solution.py:324
  1994.3 874.2 %reduce-scatter.51.cloned.1.call-start = ((), (), s32[]{:S(2)}) async-start(), calls=%async_computation.24 | async-start | bytes 11796480 | tf_op jit(solution)/shard_map/reduce_scatter | solution.py:324
  (439 other events, 7366.8 us)
Sparse Core Ops, SparseCore 0:
  9.5 67.2 all-gather.15
  78.4 171.6 all-gather.13
  251.7 227.8 all-gather.17
  481.0 227.8 all-gather.19
  1345.5 19.8 reduce-scatter.66
  1367.8 20.7 reduce-scatter.58
  1391.8 25.5 reduce-scatter.52
  1419.9 27.9 reduce-scatter.62
  1450.6 77.9 reduce-scatter.40
  1531.0 202.9 reduce-scatter.36
  1736.6 257.6 reduce-scatter.44
  1996.7 257.6 reduce-scatter.48
  2256.8 19.4 reduce-scatter.56
  2278.4 19.6 reduce-scatter.68
  2300.2 17.8 reduce-scatter.60
  2320.7 20.3 reduce-scatter.54
  2343.8 21.4 reduce-scatter.64
  2367.5 47.2 reduce-scatter.42
  2417.0 122.8 reduce-scatter.38
  2542.2 161.6 reduce-scatter.46
  2706.3 162.1 reduce-scatter.50
where the time goes:
time: 2890 us; the launch traced here: 2880 us
  waiting for transfers between devices  1770 us (61%)
  matrix products  528 us (18%)
  other arithmetic  331 us (11%)
  local copies, waits for them, and re-layouts  179 us (6%)
  blocking collectives  39.8 us (1%)
    reduce_scatter x4, waiting for transfers between devices, reduce_matrix(): lax.psum_scatter(matrix_terms(left, right).astype(jnp.bfloat16), 'shard',...  648 us
    reduce_scatter x4, waiting for transfers between devices, reduce_matrix(): lax.psum_scatter(group_sum, 'replica', scatter_dimension=0, tiled=True)  491 us
    all_gather x1, waiting for transfers between devices, per_device(): lax.all_gather(own_shards[7], 'shard', axis=1, tiled=True)  202 us
    all_gather x1, waiting for transfers between devices, per_device(): lax.all_gather(own_shards[5], 'shard', axis=1, tiled=True)  175 us
    all_gather x1, waiting for transfers between devices, per_device(): lax.all_gather(own_shards[0], 'shard', axis=1, tiled=True)  165 us
    unnamed x935, local copies, waits for them, and re-layouts  86.1 us
    another operation x4, other arithmetic, matrix_terms(): return jnp.stack([image_part, text_part], 1)  82.3 us
    dot_general x6, matrix products, backward_pass(): jnp.einsum('snd,fd->snf', mlp_grad, w_down[token_stream], preferred_eleme...  76.4 us
  transfers between devices with their start and end apart: 25, of which 17 were waited for; matrix products, arithmetic and copies ran while one was open for 16% of the time, Pallas kernels for 0%

commit v1 on v0

v1 whole, which is shorter than its diff:
```python
import jax
import jax.numpy as jnp
from jax import lax
from jax.sharding import PartitionSpec as P

IMG = 64
norm_eps = 1e-06
BF = jnp.bfloat16
F32 = jnp.float32


def dot(spec, a, b):
    return jnp.einsum(spec, a, b, preferred_element_type=F32)


def near(x):
    return lax.ppermute(x, "shard", [(i, i ^ 1) for i in range(4)])


def far(x):
    return lax.ppermute(x, "shard", [(i, i ^ 2) for i in range(4)])


def across(x):
    return lax.ppermute(x, "shard", [(i, i ^ 3) for i in range(4)])


def mate(x):
    count = lax.axis_size("replica")
    return lax.ppermute(x, "replica", [(i, i ^ 1) for i in range(count)])


def gather_two(x):
    return jnp.concatenate([x, near(x)], 0)


def gather_four(x):
    other = far(x)
    return jnp.concatenate([x, near(x), other, near(other)], 0)


def scatter_two(parts):
    own = parts.shape[0] // 2
    return parts[:own] + near(parts[own:].astype(BF)).astype(F32)


def scatter_four(parts):
    own = parts.shape[0] // 4
    away = parts[2 * own : 3 * own] + near(parts[3 * own :].astype(BF)).astype(F32)
    away = far(away.astype(BF))
    here = parts[:own] + near(parts[own : 2 * own].astype(BF)).astype(F32)
    return here + away.astype(F32)


def normalise(x):
    centred = x - jnp.mean(x, -1, keepdims=True)
    inverse = lax.rsqrt(jnp.mean(centred * centred, -1, keepdims=True) + norm_eps)
    return centred * inverse, inverse


def normalise_back(f, normed, inverse):
    return inverse * (
        f - jnp.mean(f, -1, keepdims=True) - normed * jnp.mean(f * normed, -1, keepdims=True)
    )


gelu_a = (2.0 / jnp.pi) ** 0.5
gelu_b = 0.044715


def gelu(v):
    return 0.5 * v * (1.0 + jnp.tanh(gelu_a * (v + gelu_b * v * v * v)))


def gelu_slope(v):
    t = jnp.tanh(gelu_a * (v + gelu_b * v * v * v))
    return 0.5 * (1.0 + t) + 0.5 * v * (1.0 - t * t) * gelu_a * (1.0 + 3.0 * gelu_b * v * v)


def split_rows(x):
    return (x[:, :IMG], x[:, IMG:])


def key_mask(length, padded):
    return jnp.where(jnp.arange(padded) < length, 0.0, -1e30).astype(F32)


def attention(u, gains, length):
    queries, keys, values = [], [], []
    for st in range(2):
        pair = u[st][:, :, :2]
        normed = pair * lax.rsqrt(jnp.mean(pair * pair, -1, keepdims=True) + norm_eps)
        normed = (normed * gains[st][:, None, :]).astype(BF)
        queries.append(normed[:, :, 0])
        keys.append(normed[:, :, 1])
        values.append(u[st][:, :, 2].astype(BF))
    q, k, v = (jnp.concatenate(t, 1) for t in (queries, keys, values))
    n, padded, heads, hd = q.shape
    scores = dot("sqhd,skhd->shqk", q, k) * hd**-0.5 + key_mask(length, padded)
    exponent = jnp.exp(scores)
    total = jnp.sum(exponent, -1, keepdims=True)
    probs = (exponent / total).astype(BF)
    attended = dot("shqk,skhd->sqhd", probs, v).astype(BF)
    return attended.reshape(n, padded, heads * hd), (q, k, v, jnp.log(total))


def attention_back(attended_grad, u, gains, saved, length):
    q, k, v, log_total = saved
    n, padded, heads, hd = q.shape
    scale = hd**-0.5
    scores = dot("sqhd,skhd->shqk", q, k) * scale + key_mask(length, padded)
    exact = jnp.exp(scores - log_total)
    grad = attended_grad.reshape(n, padded, heads, hd)
    value_grad = dot("shqk,sqhd->skhd", exact.astype(BF), grad)
    prob_grad = dot("sqhd,skhd->shqk", grad, v)
    delta = jnp.sum(prob_grad * exact, -1, keepdims=True)
    score_grad = (exact * (prob_grad - delta)).astype(BF)
    query_grad = dot("shqk,skhd->sqhd", score_grad, k) * scale
    key_grad = dot("shqk,sqhd->skhd", score_grad, q) * scale
    projected_grad, gain_grad = [], []
    for st, part in enumerate(zip(split_rows(query_grad), split_rows(key_grad), split_rows(value_grad))):
        pair = u[st][:, :, :2]
        t = jnp.stack(part[:2], 2)
        r = lax.rsqrt(jnp.mean(pair * pair, -1, keepdims=True) + norm_eps)
        g = gains[st][:, None, :]
        back = r * g * t - pair * (r * r * r) * jnp.mean(pair * g * t, -1, keepdims=True)
        gain_grad.append(jnp.sum(t * pair * r, (0, 1, 3)))
        whole = jnp.concatenate([back, part[2][:, :, None]], 2).astype(BF)
        projected_grad.append(whole.reshape(n, whole.shape[1], 3 * heads * hd))
    return projected_grad, gain_grad


def forward(x, mod, w, length):
    us, mixeds, saved = [], [], {}
    keep = {"x": x, "mod": mod}
    hidden = []
    hd = w["gain"].shape[-1]
    for st in range(2):
        normed, _ = normalise(x[st].astype(F32))
        h = (normed * (1.0 + mod[:, st, 1][:, None]) + mod[:, st, 0][:, None]).astype(BF)
        h = gather_two(h)
        hidden.append(h)
        p = dot("nrd,dk->nrk", h, w["qkv"][st]) + w["b_qkv"][st]
        us.append(p.reshape(p.shape[0], p.shape[1], 3, -1, hd))
    keep["hidden"], keep["u"] = hidden, us
    attended, keep["att"] = attention(us, w["gain"], length)
    attended = split_rows(attended)
    keep["attended"] = attended
    keep["branch"], keep["mixed"], keep["hidden_mlp"], keep["pre"], keep["act"], keep["mlp"] = [], [], [], [], [], []
    outs = []
    for st in range(2):
        branch = scatter_two(dot("nrk,kd->nrd", attended[st], w["out"][st])) + w["b_out"][st]
        mixed = x[st].astype(F32) + mod[:, st, 2][:, None] * branch
        normed, _ = normalise(mixed)
        h = (normed * (1.0 + mod[:, st, 4][:, None]) + mod[:, st, 3][:, None]).astype(BF)
        h = gather_four(h)
        pre = dot("nrd,df->nrf", h, w["fc1"][st]) + w["b_fc1"][st]
        act = gelu(pre).astype(BF)
        mlp = scatter_four(dot("nrf,fd->nrd", act, w["fc2"][st])) + w["b_fc2"][st]
        outs.append(mixed + mod[:, st, 5][:, None] * mlp)
        for name, value in (("branch", branch), ("mixed", mixed), ("hidden_mlp", h), ("pre", pre), ("act", act), ("mlp", mlp)):
            keep[name].append(value)
    return outs, keep


def backward(up, keep, w, length):
    mod = keep["mod"]
    mixed_grads, late, right, small = [], [], {}, {}
    right["mlp"], right["pre"], right["branch"] = [], [], []
    attended_grads, gates = [], []
    small["fc2"], small["fc1"], small["out"] = [], [], []
    for st in range(2):
        mlp_grad = (mod[:, st, 5][:, None] * up[st]).astype(BF)
        small["fc2"].append(jnp.sum(mlp_grad.astype(F32), (0, 1)))
        gate = jnp.sum(keep["mlp"][st] * up[st], 1)
        mlp_grad = gather_four(mlp_grad)
        act_grad = dot("nrd,fd->nrf", mlp_grad, w["fc2"][st])
        pre_grad = (act_grad * gelu_slope(keep["pre"][st])).astype(BF)
        small["fc1"].append(jnp.sum(pre_grad.astype(F32), (0, 1)))
        h_grad = scatter_four(dot("nrf,df->nrd", pre_grad, w["fc1"][st]))
        normed, inverse = normalise(keep["mixed"][st])
        mixed_grad = up[st] + normalise_back(h_grad * (1.0 + mod[:, st, 4][:, None]), normed, inverse)
        late.append((jnp.sum(h_grad, 1), jnp.sum(h_grad * normed, 1), gate))
        mixed_grads.append(mixed_grad)
        right["mlp"].append(mlp_grad)
        right["pre"].append(pre_grad)
        branch_grad = (mod[:, st, 2][:, None] * mixed_grad).astype(BF)
        gates.append(jnp.sum(keep["branch"][st] * mixed_grad, 1))
        small["out"].append(jnp.sum(branch_grad.astype(F32), (0, 1)))
        branch_grad = gather_two(branch_grad)
        right["branch"].append(branch_grad)
        attended_grads.append(dot("nrd,kd->nrk", branch_grad, w["out"][st]).astype(BF))
    attended_grad = jnp.concatenate(attended_grads, 1)
    right["qkv"], small["gain"] = attention_back(attended_grad, keep["u"], w["gain"], keep["att"], length)
    small["qkv"] = [jnp.sum(t.astype(F32), (0, 1)) for t in right["qkv"]]
    input_grads, mod_grads = [], []
    for st in range(2):
        h_grad = scatter_two(dot("nrk,dk->nrd", right["qkv"][st], w["qkv"][st]))
        normed, inverse = normalise(keep["x"][st].astype(F32))
        input_grads.append(mixed_grads[st] + normalise_back(h_grad * (1.0 + mod[:, st, 1][:, None]), normed, inverse))
        mod_grads.append(jnp.stack([jnp.sum(h_grad, 1), jnp.sum(h_grad * normed, 1), gates[st], *late[st]], 1))
    return input_grads, jnp.stack(mod_grads, 1), small, right


def place(pieces, slots, count):
    whole = jnp.zeros((count,) + pieces[0].shape, pieces[0].dtype)
    for piece, slot in zip(pieces, slots):
        whole = lax.dynamic_update_index_in_dim(whole, piece, slot, 0)
    return whole


def take(x, index, axis):
    return lax.dynamic_index_in_dim(x, index, axis, keepdims=False)


def halves(mine, parity):
    direct = far(take(mine, parity, 0))
    relayed = mate(direct)
    return tuple(jnp.where(parity == st, direct, relayed) for st in range(2))


def prepare(w_qkv, b_qkv, gain, w_out, b_out, w_fc1, b_fc1, w_fc2, b_fc2):
    sid = lax.axis_index("shard")
    core = sid % 2
    parity = lax.axis_index("replica") % 2
    rows, width = w_qkv.shape[1], w_qkv.shape[2]
    part = width // 12
    vectors = (b_qkv, b_out, b_fc1, b_fc2, gain.reshape(2, -1))
    packed = lax.all_gather(jnp.concatenate(vectors, 1), "shard", axis=0)
    unpacked, at = [], 0
    for vector in vectors:
        piece = packed[:, :, at : at + vector.shape[1]].astype(F32)
        at += vector.shape[1]
        unpacked.append(piece)
    flat = [jnp.swapaxes(piece, 0, 1).reshape(2, -1) for piece in unpacked[:4]]
    hd = gain.shape[2] * 4
    gains = jnp.transpose(unpacked[4].reshape(4, 2, 2, -1), (1, 2, 0, 3)).reshape(2, 2, hd)
    w = {"gain": gains, "b_out": flat[1], "b_fc2": flat[3], "b_fc1": b_fc1.astype(F32)}
    w["b_qkv"] = take(flat[0].reshape(2, 3, 2, 2, part), core, 3).reshape(2, 3 * 2 * part)
    heads = w_qkv.reshape(2, rows, 3, 2, 2, part)
    own = take(heads, core, 4)
    beside = near(take(heads, 1 - core, 4))
    qkv_parts = []
    for j in range(3):
        far_own = halves(own[:, :, j], parity)
        far_beside = halves(beside[:, :, j], parity)
        qkv_parts.append((far_own, far_beside))
    slots = (sid, sid ^ 1, sid ^ 2, sid ^ 3)
    w["qkv"] = []
    for st in range(2):
        far_own = jnp.stack([qkv_parts[j][0][st] for j in range(3)], 1)
        far_beside = jnp.stack([qkv_parts[j][1][st] for j in range(3)], 1)
        whole = place((own[st], beside[st], far_own, far_beside), slots, 4)
        w["qkv"].append(whole.reshape(4 * rows, 3 * 2 * part))
    far_out = halves(w_out, parity)
    row_pair = sid // 2
    w["out"] = [
        place((w_out[st], far_out[st]), (row_pair, 1 - row_pair), 2).reshape(2 * rows, -1) for st in range(2)
    ]
    columns = w_fc1.reshape(2, rows, 4, -1)
    blocks = [take(columns, slots[j], 2) for j in range(4)]
    beside = near(blocks[1])
    behind = [blocks[2], blocks[3]]
    behind, far_out = lax.optimization_barrier((behind, far_out))
    direct = [far(take(behind[0], parity, 0)), across(take(behind[1], parity, 0))]
    relayed = [mate(t) for t in direct]
    w["fc1"] = []
    for st in range(2):
        away = [jnp.where(parity == st, d, m) for d, m in zip(direct, relayed)]
        w["fc1"].append(place((blocks[0][st], beside[st], *away), slots, 4).reshape(4 * rows, -1))
    w["fc2"] = [w_fc2[0], w_fc2[1]]
    return w


def weight_terms(left, right):
    total = None
    for a, b in zip(left, right):
        term = dot("nrd,nre->de", a, b)
        total = term if total is None else total + term
    return total


def over_replicas(x):
    return lax.psum_scatter(x, "replica", scatter_dimension=0, tiled=True)


def per_device(block_input, modulation, w_qkv, b_qkv, qk_gain, w_out, b_out, w_fc1, b_fc1, w_fc2, b_fc2, cotangent):
    section = lax.axis_index("section")
    first = section == 0
    sid = lax.axis_index("shard")
    core, row_pair = sid % 2, sid // 2
    count = lax.axis_size("replica")
    rid = lax.axis_index("replica")
    length = block_input.shape[2]
    padded = (length + 15) // 16 * 16
    w = prepare(w_qkv[0], b_qkv[0], qk_gain[0], w_out[0], b_out[0], w_fc1[0], b_fc1[0], w_fc2[0], b_fc2[0])

    def padding(x):
        return jnp.pad(x, ((0, 0), (0, 0), (0, padded - length), (0, 0)))

    def streams(x):
        return list(split_rows(x))

    def choose(a, b):
        return jax.tree.map(lambda p, q: jnp.where(first, p, q), a, b)

    def relay(x, pairs):
        return [lax.ppermute(t.astype(BF), "section", pairs) for t in x]

    block_input = padding(block_input)
    cotangent = padding(cotangent)
    mod = modulation[0]
    middle_mod = jnp.where(first, mod[1], mod[0])
    up_pair, down_pair = [(0, 1)], [(1, 0)]

    out0, keep0 = forward(streams(block_input[0]), mod[0], w, length)
    got = relay(out0, up_pair)
    out1, keep1 = forward(choose(streams(block_input[1]), got), middle_mod, w, length)
    got = relay(out1, up_pair)
    out2, keep2 = forward(got, mod[1], w, length)

    def zero_unless(cond, x):
        return [jnp.where(cond, t.astype(F32), 0.0) for t in x]

    grad0, mod_grad0, small0, right0 = backward(zero_unless(~first, streams(cotangent[0])), keep1, w, length)
    got = relay(grad0, down_pair)
    up = choose([t.astype(F32) for t in got], [t.astype(F32) for t in streams(cotangent[1])])
    keep_mid = choose(keep0, keep2)
    grad1, mod_grad1, small1, right1 = backward(up, keep_mid, w, length)
    got = relay(grad1, down_pair)
    grad2, mod_grad2, small2, right2 = backward(zero_unless(first, got), keep1, w, length)

    ends = choose(right2, right0)

    def terms(left, right, st):
        return weight_terms((keep_mid[left][st], keep1[left][st]), (right1[right][st], ends[right][st])).astype(BF)

    fc2 = jnp.stack([over_replicas(terms("act", "mlp", st)) for st in range(2)]).astype(F32)
    fc1 = []
    for st in range(2):
        t = terms("hidden_mlp", "pre", st)
        d, cols = t.shape
        t = jnp.swapaxes(t.reshape(4, count, -1, cols), 0, 1).reshape(d, cols)
        fc1.append(over_replicas(t).reshape(4, -1, cols))
    fc1 = jnp.stack(fc1, 1)
    own = take(fc1, sid, 0)
    moved = [own] + [send(take(fc1, sid ^ j, 0)) for j, send in ((1, near), (2, far), (3, across))]
    fc1 = place(moved, [sid ^ j for j in range(4)], 4)
    fc1 = jnp.transpose(fc1, (1, 2, 0, 3)).reshape(2, fc1.shape[2], -1).astype(F32)

    out, qkv = [], []
    for st in range(2):
        t = terms("attended", "branch", st)
        t = t.reshape(2, -1, t.shape[1])
        t = take(t, row_pair, 0).astype(F32) + far(take(t, 1 - row_pair, 0)).astype(F32)
        out.append(over_replicas(t.astype(BF)))
    out = jnp.stack(out).astype(F32)
    for st in range(2):
        t = terms("hidden", "qkv", st)
        cols = t.shape[1]
        t = t.reshape(2, -1, cols)
        t = take(t, row_pair, 0).astype(F32) + far(take(t, 1 - row_pair, 0)).astype(F32)
        t = jnp.swapaxes(t.astype(BF).reshape(2, count, -1, cols), 0, 1).reshape(-1, cols)
        qkv.append(over_replicas(t).reshape(2, -1, cols))
    qkv = jnp.stack(qkv, 1)
    own = take(qkv, core, 0)
    other = near(take(qkv, 1 - core, 0))
    qkv = place((own, other), (core, 1 - core), 2)
    rows = qkv.shape[2]
    qkv = qkv.reshape(2, 2, rows, 6, -1)
    qkv = jnp.transpose(qkv, (1, 2, 3, 0, 4)).reshape(2, rows, -1).astype(F32)

    small = jax.tree.map(lambda a, b, c: a + b + c, small0, small1, small2)
    pieces = []
    for st in range(2):
        cores = small["qkv"][st].reshape(6, 1, -1)
        cores = jnp.where(jnp.arange(2).reshape(1, 2, 1) == core, cores, 0.0).reshape(-1)
        quarter = small["fc1"][st].reshape(1, -1)
        quarter = jnp.where(jnp.arange(4).reshape(4, 1) == sid, quarter, 0.0).reshape(-1)
        pieces.append(jnp.concatenate([cores, small["out"][st], quarter, small["fc2"][st], small["gain"][st].reshape(-1)]))
    sizes = [w_qkv.shape[3], w_out.shape[3], w_fc1.shape[3], w_fc2.shape[3], 2 * w["gain"].shape[-1]]
    summed = lax.psum(jnp.stack(pieces), ("shard", "replica"))
    place_id = sid * count + rid
    vectors, at = [], 0
    for size in sizes:
        vectors.append(summed[:, at : at + size])
        at += size

    def own_block(x, axis):
        size = x.shape[axis] // (4 * count)
        return lax.dynamic_slice_in_dim(x, place_id * size, size, axis)

    blocks = [own_block(v, 1)[None] for v in vectors[:4]]
    gain = own_block(vectors[4].reshape(2, 2, -1), 2)[None]

    def joined(x):
        return jnp.concatenate(x, 1)[:, :length]

    activations = jnp.stack([joined(choose(out0, out1)), joined(choose(out1, out2))]).astype(BF)
    input_grads = jnp.stack([joined(choose(grad1, grad0)), joined(choose(grad2, grad1))])
    modulation_grad = jnp.stack([choose(mod_grad1, mod_grad0), choose(mod_grad2, mod_grad1)])
    return (
        activations[None],
        input_grads[None],
        modulation_grad[None],
        qkv[None],
        blocks[0],
        gain,
        out[None],
        blocks[1],
        fc1[None],
        blocks[2],
        fc2[None],
        blocks[3],
    )


def solution(mesh):
    every = ("shard", "replica")
    return jax.shard_map(
        per_device,
        mesh=mesh,
        in_specs=(
            P(None, every, None, None),
            P("section", None, every, None, None, None),
            P("section", None, "shard", None),
            P("section", None, "shard"),
            P("section", None, None, "shard"),
            P("section", None, "shard", None),
            P("section", None, "shard"),
            P("section", None, "shard", None),
            P("section", None, "shard"),
            P("section", None, "shard", None),
            P("section", None, "shard"),
            P(None, every, None, None),
        ),
        out_specs=(
            P("section", None, every, None, None),
            P("section", None, every, None, None),
            P("section", None, every, None, None, None),
            P("section", None, every, None),
            P("section", None, every),
            P("section", None, None, every),
            P("section", None, every, None),
            P("section", None, every),
            P("section", None, every, None),
            P("section", None, every),
            P("section", None, every, None),
            P("section", None, every),
        ),
        check_vma=False,
    )
```

time: 2890 us -> 1720 us (0.60)
  waiting for transfers between devices: 1770 us -> 560 us
  local copies, waits for them, and re-layouts: 179 us -> 464 us
  matrix products: 528 us -> 324 us
  other arithmetic: 331 us -> 217 us
  starting transfers between devices: 12.9 us -> 82.1 us
    reduce_scatter x8, waiting for transfers between devices: 1140 us -> 176 us  [over_replicas(): return lax.psum_scatter(x, 'replica', scatter_dimension=0, tiled=True)]
    all_gather x4 -> x0, waiting for transfers between devices: 562 us -> none  [the longest x1 202 us: per_device(): lax.all_gather(own_shards[7], 'shard', axis=1, tiled=True)]
    ppermute x4 -> x132, waiting for transfers between devices: 25.7 us -> 383 us  [the longest x37 312 us: far(): return lax.ppermute(x, 'shard', [(i, i ^ 2) for i in range(4)])]
    dot_general x77 -> x83, matrix products: 528 us -> 324 us  [dot(): return jnp.einsum(spec, a, b, preferred_element_type=F32)]
    another operation x61 -> x17, other arithmetic: 146 us -> 13.6 us  [the longest x4 82.3 us: matrix_terms(): return jnp.stack([image_part, text_part], 1)]
    dynamic_update_slice x0 -> x18, local copies, waits for them, and re-layouts: none -> 73.1 us  [place(): whole = lax.dynamic_update_index_in_dim(whole, piece, slot, 0)]
    ppermute x4 -> x132, starting transfers between devices: 10.8 us -> 80.9 us  [the longest x37 38.8 us: far(): return lax.ppermute(x, 'shard', [(i, i ^ 2) for i in range(4)])]
    slice x3 -> x48, local copies, waits for them, and re-layouts: 9.98 us -> 62 us  [the longest x4 19.7 us: prepare(): whole = place((own[st], beside[st], far_own, far_beside), slots, 4)]
  transfers between devices with their start and end apart: 25 -> 141, of which waited for: 17 -> 45; matrix products, arithmetic and copies ran while one was open for 16% -> 51% of each run, Pallas kernels for 0% -> 0%
where the time goes in v1:
time: 1720 us; the launch traced here: 1710 us
  waiting for transfers between devices  560 us (33%)
  local copies, waits for them, and re-layouts  464 us (27%)
  matrix products  324 us (19%)
  other arithmetic  217 us (13%)
  starting transfers between devices  82.1 us (5%)
  blocking collectives  38.4 us (2%)
  between operations  23.4 us (1%)
    dot_general x83, matrix products, dot(): return jnp.einsum(spec, a, b, preferred_element_type=F32)  324 us
    ppermute x37, waiting for transfers between devices, far(): return lax.ppermute(x, 'shard', [(i, i ^ 2) for i in range(4)])  312 us
    reduce_scatter x8, waiting for transfers between devices, over_replicas(): return lax.psum_scatter(x, 'replica', scatter_dimension=0, tiled=True)  176 us
    unnamed x1164, local copies, waits for them, and re-layouts  102 us
    dynamic_update_slice x18, local copies, waits for them, and re-layouts, place(): whole = lax.dynamic_update_index_in_dim(whole, piece, slot, 0)  73.1 us
    ppermute x37, starting transfers between devices, far(): return lax.ppermute(x, 'shard', [(i, i ^ 2) for i in range(4)])  38.8 us
    all_gather x1, blocking collectives, prepare(): packed = lax.all_gather(jnp.concatenate(vectors, 1), 'shard', axis=0)  38.4 us
    dynamic_slice x8, local copies, waits for them, and re-layouts, take(): return lax.dynamic_index_in_dim(x, index, axis, keepdims=False)  36.4 us
  transfers between devices with their start and end apart: 141, of which 45 were waited for; matrix products, arithmetic and copies ran while one was open for 51% of the time, Pallas kernels for 0%

profile of v1, /device:TPU:0, one launch (start us, length us, event | category | flops | bytes accessed | tf_op | source)
XLA Modules:
  0.0 1709.0 jit_solution(17332044870322234634)
XLA Ops:
  13.4 10.3 copy.238
  50.2 38.4 %all-gather.1 = bf16[4,2,3488]{2,1,0:T(2,128)(2,1)S(1)} all-gather(bf16[1,2,3488]{2,1,0:T(2,128)(2,1)S(1)} %bitcast.667), channel_id=2, replica_groups=mesh['section'=2,'shard'=4,'replica'=4] {'shard'}, dimensions={0}, use_global_device_ids=true | all-gather | bytes 69760 | tf_op jit(solution)/shard_map/all_gather | solution.py:229
  106.7 12.6 copy.260
  213.0 21.3 %collective-permute-done.16 = bf16[384,1536]{1,0:T(8,128)(2,1)S(1)} collective-permute-done((bf16[384,1536]{1,0:T(8,128)(2,1)}, bf16[384,1536]{1,0:T(8,128)(2,1)S(1)}, u32[]{:S(2)}, u32[]{:S(2)}) %collective-permute-start.16) | collective-permute-done | bytes 1179680 | tf_op jit(solution)/shard_map/ppermute | solution.py:30
  262.7 12.2 collective-permute-done.10
  275.4 10.3 collective-permute-done.8
  290.1 9.2 collective-permute-done.9
  304.0 16.0 reshape.1784
  320.9 17.8 %collective-permute-done.24 = bf16[384,1536]{1,0:T(8,128)(2,1)} collective-permute-done((bf16[384,1536]{1,0:T(8,128)(2,1)}, bf16[384,1536]{1,0:T(8,128)(2,1)}, u32[]{:S(2)}, u32[]{:S(2)}) %collective-permute-start.24) | collective-permute-done | bytes 1179680 | tf_op jit(solution)/shard_map/ppermute | solution.py:25
  357.3 16.0 reshape.1783
  435.4 9.0 collective-permute-done.33
  464.1 11.7 collective-permute-done.37
  639.2 11.9 collective-permute-done.53
  848.2 11.4 convert_reduce_fusion.4
  868.9 11.9 collective-permute-done.102
  1021.6 10.0 collective-permute-done.120
  1080.0 26.9 %collective-permute-done.128 = bf16[384,1536]{1,0:T(8,128)(2,1)S(1)} collective-permute-done((bf16[384,1536]{1,0:T(8,128)(2,1)S(1)}, bf16[384,1536]{1,0:T(8,128)(2,1)S(1)}, u32[]{:S(2)}, u32[]{:S(2)}) %collective-permute-start.128) | collective-permute-done | bytes 1179680 | tf_op jit(solution)/shard_map/ppermute | solution.py:21
  1155.4 76.8 %collective-permute-done.124 = bf16[768,2304]{1,0:T(8,128)(2,1)S(1)} collective-permute-done((bf16[768,2304]{1,0:T(8,128)(2,1)S(1)}, bf16[768,2304]{1,0:T(8,128)(2,1)S(1)}, u32[]{:S(2)}, u32[]{:S(2)}) %collective-permute-start.124) | collective-permute-done | bytes 3538976 | tf_op jit(solution)/shard_map/ppermute | solution.py:21
  1235.7 11.6 fusion.214
  1258.1 76.0 %collective-permute-done.125 = bf16[768,2304]{1,0:T(8,128)(2,1)S(1)} collective-permute-done((bf16[768,2304]{1,0:T(8,128)(2,1)S(1)}, bf16[768,2304]{1,0:T(8,128)(2,1)S(1)}, u32[]{:S(2)}, u32[]{:S(2)}) %collective-permute-start.125) | collective-permute-done | bytes 3538976 | tf_op jit(solution)/shard_map/ppermute | solution.py:21
  1351.3 10.0 fusion.96
  1455.2 84.7 %reduce-scatter.21.cloned.1.call-done = bf16[384,1536]{1,0:T(8,128)(2,1)} async-done(((bf16[1536,1536]{1,0:T(8,128)(2,1)}), bf16[384,1536]{1,0:T(8,128)(2,1)}) %reduce-scatter.21.cloned.1.call-update) | async-done | bytes 1179664 | tf_op jit(solution)/shard_map/reduce_scatter | solution.py:284
  1539.9 87.9 %reduce-scatter.23.cloned.1.call-done = bf16[384,1536]{1,0:T(8,128)(2,1)} async-done(((bf16[1536,1536]{1,0:T(8,128)(2,1)}), bf16[384,1536]{1,0:T(8,128)(2,1)}) %reduce-scatter.23.cloned.1.call-update) | async-done | bytes 1179664 | tf_op jit(solution)/shard_map/reduce_scatter | solution.py:284
  1647.9 16.4 dynamic_update_slice.107
  (1994 shorter events, 1065.5 us)
Async XLA Ops:
  8.0 1404.6 %all-reduce.4.cloned.1.call-start = ((), (), s32[]{:S(2)}) async-start(), calls=%async_computation.10 | async-start | bytes 223232 | tf_op jit(solution)/shard_map/psum | solution.py:382
  10.4 171.6 %collective-permute-start.15 = (bf16[384,1536]{1,0:T(8,128)(2,1)}, bf16[384,1536]{1,0:T(8,128)(2,1)}, u32[]{:S(2)}, u32[]{:S(2)}) collective-permute-start(bf16[384,1536]{1,0:T(8,128)(2,1)} %dynamic-slice_bitcast_fusion.8), channel_id=1, source_target_pairs={{0,8},{4,12},{8,0},{12,4},{1,9},{5,13},{9,1},{13,5},{2,10},{6,14},... | collective-permute-start | bytes 3538952 | tf_op jit(solution)/shard_map/ppermute | solution.py:21
  36.9 206.7 %collective-permute-start.1 = (bf16[2,384,3,2,384]{4,1,3,2,0:T(8,128)(2,1)}, bf16[2,384,3,2,384]{4,1,3,2,0:T(8,128)(2,1)}, u32[]{:S(2)}, u32[]{:S(2)}) collective-permute-start(bf16[2,384,3,2,384]{4,1,3,2,0:T(8,128)(2,1)} %bitcast.643), channel_id=1, source_target_pairs={{0,4},{4,0},{8,12},{12,8},{1,5},{5,1},{9,13},{13,9},{2,6},{6,2},{1... | collective-permute-start | bytes 10616840 | tf_op jit(solution)/shard_map/ppermute | solution.py:17
  46.2 114.3 %collective-permute-start.6 = (bf16[384,2,384]{2,0,1:T(8,128)(2,1)}, bf16[384,2,384]{2,0,1:T(8,128)(2,1)}, u32[]{:S(2)}, u32[]{:S(2)}) collective-permute-start(bf16[384,2,384]{2,0,1:T(8,128)(2,1)} %dynamic-slice_bitcast_fusion.12), channel_id=1, source_target_pairs={{0,8},{4,12},{8,0},{12,4},{1,9},{5,13},{9,1},{13,5},{2,10},{6,14},... | collective-permute-start | bytes 1769480 | tf_op jit(solution)/shard_map/ppermute | solution.py:21
  47.1 133.9 %collective-permute-start.4 = (bf16[384,2,384]{2,0,1:T(8,128)(2,1)}, bf16[384,2,384]{2,0,1:T(8,128)(2,1)}, u32[]{:S(2)}, u32[]{:S(2)}) collective-permute-start(bf16[384,2,384]{2,0,1:T(8,128)(2,1)} %dynamic-slice_bitcast_fusion.13), channel_id=1, source_target_pairs={{0,8},{4,12},{8,0},{12,4},{1,9},{5,13},{9,1},{13,5},{2,10},{6,14},... | collective-permute-start | bytes 1769480 | tf_op jit(solution)/shard_map/ppermute | solution.py:21
  50.0 132.1 %collective-permute-start.2 = (bf16[384,2,384]{2,0,1:T(8,128)(2,1)}, bf16[384,2,384]{2,0,1:T(8,128)(2,1)}, u32[]{:S(2)}, u32[]{:S(2)}) collective-permute-start(bf16[384,2,384]{2,0,1:T(8,128)(2,1)} %dynamic-slice_bitcast_fusion.14), channel_id=1, source_target_pairs={{0,8},{4,12},{8,0},{12,4},{1,9},{5,13},{9,1},{13,5},{2,10},{6,14},... | collective-permute-start | bytes 1769480 | tf_op jit(solution)/shard_map/ppermute | solution.py:21
  209.4 338.5 %collective-permute-start.80 = (bf16[1,160,1536]{2,1,0:T(8,128)(2,1)}, bf16[1,160,1536]{2,1,0:T(8,128)(2,1)}, u32[]{:S(2)}, u32[]{:S(2)}) collective-permute-start(bf16[1,160,1536]{2,1,0:T(8,128)(2,1)} %get-tuple-element.212), channel_id=1, source_target_pairs={{0,8},{4,12},{8,0},{12,4},{1,9},{5,13},{9,1},{13,5},{2,10},{6,14},... | collective-permute-start | bytes 1474568 | tf_op jit(solution)/shard_map/ppermute | solution.py:21
  211.1 414.2 %collective-permute-start.79 = (bf16[1,160,1536]{2,1,0:T(8,128)(2,1)}, bf16[1,160,1536]{2,1,0:T(8,128)(2,1)}, u32[]{:S(2)}, u32[]{:S(2)}) collective-permute-start(bf16[1,160,1536]{2,1,0:T(8,128)(2,1)} %get-tuple-element.212), channel_id=1, source_target_pairs={{0,4},{4,0},{8,12},{12,8},{1,5},{5,1},{9,13},{13,9},{2,6},{6,2},{1... | collective-permute-start | bytes 1474568 | tf_op jit(solution)/shard_map/ppermute | solution.py:17
  320.6 93.3 %collective-permute-start.23 = (bf16[384,1536]{1,0:T(8,128)(2,1)}, bf16[384,1536]{1,0:T(8,128)(2,1)}, u32[]{:S(2)}, u32[]{:S(2)}) collective-permute-start(bf16[384,1536]{1,0:T(8,128)(2,1)} %collective-permute-done.22), channel_id=1, source_target_pairs={{0,1},{1,0},{2,3},{3,2},{4,5},{5,4},{6,7},{7,6},{8,9},{9,8},{10,11... | collective-permute-start | bytes 3538952 | tf_op jit(solution)/shard_map/ppermute | solution.py:30
  338.7 79.2 %collective-permute-start.25 = (bf16[384,1536]{1,0:T(8,128)(2,1)}, bf16[384,1536]{1,0:T(8,128)(2,1)}, u32[]{:S(2)}, u32[]{:S(2)}) collective-permute-start(bf16[384,1536]{1,0:T(8,128)(2,1)} %collective-permute-done.24), channel_id=1, source_target_pairs={{0,1},{1,0},{2,3},{3,2},{4,5},{5,4},{6,7},{7,6},{8,9},{9,8},{10,11... | collective-permute-start | bytes 3538952 | tf_op jit(solution)/shard_map/ppermute | solution.py:30
  434.7 113.1 %collective-permute-start.73 = (bf16[1,64,1536]{2,1,0:T(8,128)(2,1)}, bf16[1,64,1536]{2,1,0:T(8,128)(2,1)}, u32[]{:S(2)}, u32[]{:S(2)}) collective-permute-start(bf16[1,64,1536]{2,1,0:T(8,128)(2,1)} %get-tuple-element.191), channel_id=1, source_target_pairs={{0,8},{4,12},{8,0},{12,4},{1,9},{5,13},{9,1},{13,5},{2,10},{6,14},... | collective-permute-start | bytes 589832 | tf_op jit(solution)/shard_map/ppermute | solution.py:21
  1070.9 361.2 %reduce-scatter.13.cloned.1.call-start = ((), (), s32[]{:S(2)}) async-start(), calls=%async_computation.11 | async-start | bytes 1474560 | tf_op jit(solution)/shard_map/reduce_scatter | solution.py:284
  1073.6 358.6 %reduce-scatter.15.cloned.1.call-start = ((), (), s32[]{:S(2)}) async-start(), calls=%async_computation.12 | async-start | bytes 1474560 | tf_op jit(solution)/shard_map/reduce_scatter | solution.py:284
  1108.3 326.0 %reduce-scatter.17.cloned.1.call-start = ((), (), s32[]{:S(2)}) async-start(), calls=%async_computation.13 | async-start | bytes 5898240 | tf_op jit(solution)/shard_map/reduce_scatter | solution.py:284
  1116.6 317.7 %reduce-scatter.19.cloned.1.call-start = ((), (), s32[]{:S(2)}) async-start(), calls=%async_computation.14 | async-start | bytes 5898240 | tf_op jit(solution)/shard_map/reduce_scatter | solution.py:284
  1132.9 315.8 %reduce-scatter.9.cloned.1.call-start = ((), (), s32[]{:S(2)}) async-start(), calls=%async_computation.8 | async-start | bytes 4423680 | tf_op jit(solution)/shard_map/reduce_scatter | solution.py:284
  1154.0 78.2 %collective-permute-start.124 = (bf16[768,2304]{1,0:T(8,128)(2,1)S(1)}, bf16[768,2304]{1,0:T(8,128)(2,1)S(1)}, u32[]{:S(2)}, u32[]{:S(2)}) collective-permute-start(bf16[768,2304]{1,0:T(8,128)(2,1)S(1)} %dynamic-slice_bitcast_fusion.1), channel_id=1, source_target_pairs={{0,8},{4,12},{8,0},{12,4},{1,9},{5,13},{9,1},{13,5},{2,10},{6,14},... | collective-permute-start | bytes 10616840 | tf_op jit(solution)/shard_map/ppermute | solution.py:21
  1235.3 217.1 %reduce-scatter.11.cloned.1.call-start = ((), (), s32[]{:S(2)}) async-start(), calls=%async_computation.9 | async-start | bytes 4423680 | tf_op jit(solution)/shard_map/reduce_scatter | solution.py:284
  1337.1 202.9 %reduce-scatter.21.cloned.1.call-start = ((), (), s32[]{:S(2)}) async-start(), calls=%async_computation.15 | async-start | bytes 5898240 | tf_op jit(solution)/shard_map/reduce_scatter | solution.py:284
  1347.7 280.2 %reduce-scatter.23.cloned.1.call-start = ((), (), s32[]{:S(2)}) async-start(), calls=%async_computation.16 | async-start | bytes 5898240 | tf_op jit(solution)/shard_map/reduce_scatter | solution.py:284
  1438.1 193.9 %collective-permute-start.129 = (bf16[2,96,1536]{2,1,0:T(8,128)(2,1)}, bf16[2,96,1536]{2,1,0:T(8,128)(2,1)}, u32[]{:S(2)}, u32[]{:S(2)}) collective-permute-start(bf16[2,96,1536]{2,1,0:T(8,128)(2,1)} %get-tuple-element.304), channel_id=1, source_target_pairs={{0,4},{4,0},{8,12},{12,8},{1,5},{5,1},{9,13},{13,9},{2,6},{6,2},{1... | collective-permute-start | bytes 1769480 | tf_op jit(solution)/shard_map/ppermute | solution.py:17
  1438.1 195.8 %collective-permute-start.130 = (bf16[2,96,1536]{2,1,0:T(8,128)(2,1)}, bf16[2,96,1536]{2,1,0:T(8,128)(2,1)}, u32[]{:S(2)}, u32[]{:S(2)}) collective-permute-start(bf16[2,96,1536]{2,1,0:T(8,128)(2,1)} %get-tuple-element.305), channel_id=1, source_target_pairs={{0,8},{4,12},{8,0},{12,4},{1,9},{5,13},{9,1},{13,5},{2,10},{6,14},... | collective-permute-start | bytes 1769480 | tf_op jit(solution)/shard_map/ppermute | solution.py:21
  1439.9 197.1 %collective-permute-start.131 = (bf16[2,96,1536]{2,1,0:T(8,128)(2,1)}, bf16[2,96,1536]{2,1,0:T(8,128)(2,1)}, u32[]{:S(2)}, u32[]{:S(2)}) collective-permute-start(bf16[2,96,1536]{2,1,0:T(8,128)(2,1)} %get-tuple-element.302), channel_id=1, source_target_pairs={{0,12},{4,8},{8,4},{12,0},{1,13},{5,9},{9,5},{13,1},{2,14},{6,10},... | collective-permute-start | bytes 1769480 | tf_op jit(solution)/shard_map/ppermute | solution.py:25
  1455.2 226.3 %collective-permute-start.126 = (bf16[2,96,2304]{2,1,0:T(8,128)(2,1)}, bf16[2,96,2304]{2,1,0:T(8,128)(2,1)}, u32[]{:S(2)}, u32[]{:S(2)}) collective-permute-start(bf16[2,96,2304]{2,1,0:T(8,128)(2,1)} %get-tuple-element.326), channel_id=1, source_target_pairs={{0,4},{4,0},{8,12},{12,8},{1,5},{5,1},{9,13},{13,9},{2,6},{6,2},{1... | collective-permute-start | bytes 2654216 | tf_op jit(solution)/shard_map/ppermute | solution.py:17
  (670 other events, 7091.2 us)
Sparse Core Ops, SparseCore 0:
  1071.0 241.5 all-reduce.3
Sparse Core Ops, SparseCore 1:
  1073.7 29.3 reduce-scatter.12
  1108.3 29.2 reduce-scatter.14
  1140.3 84.0 reduce-scatter.16
  1227.2 86.1 reduce-scatter.18
  1316.3 67.0 reduce-scatter.8
  1385.7 66.6 reduce-scatter.10
  1454.6 85.3 reduce-scatter.20
  1542.1 85.7 reduce-scatter.22

commit v2 on v1

v2 whole, which is shorter than its diff:
```python
import functools

import jax
import jax.numpy as jnp
from jax import lax
from jax.experimental import pallas as pl
from jax.experimental.pallas import tpu as pltpu
from jax.sharding import PartitionSpec as P

IMG = 64
norm_eps = 1e-06
BF = jnp.bfloat16
F32 = jnp.float32


def dot(spec, a, b):
    return jnp.einsum(spec, a, b, preferred_element_type=F32)


def near(x):
    return lax.ppermute(x, "shard", [(i, i ^ 1) for i in range(4)])


def far(x):
    return lax.ppermute(x, "shard", [(i, i ^ 2) for i in range(4)])


def across(x):
    return lax.ppermute(x, "shard", [(i, i ^ 3) for i in range(4)])


def mate(x):
    count = lax.axis_size("replica")
    return lax.ppermute(x, "replica", [(i, i ^ 1) for i in range(count)])


def gather_two(x):
    return jnp.concatenate([x, near(x)], 0)


def gather_four(x):
    other = far(x)
    return jnp.concatenate([x, near(x), other, near(other)], 0)


def scatter_two(parts):
    own = parts.shape[0] // 2
    return parts[:own] + near(parts[own:].astype(BF)).astype(F32)


def scatter_four(parts):
    own = parts.shape[0] // 4
    away = parts[2 * own : 3 * own] + near(parts[3 * own :].astype(BF)).astype(F32)
    away = far(away.astype(BF))
    here = parts[:own] + near(parts[own : 2 * own].astype(BF)).astype(F32)
    return here + away.astype(F32)


def normalise(x):
    centred = x - jnp.mean(x, -1, keepdims=True)
    inverse = lax.rsqrt(jnp.mean(centred * centred, -1, keepdims=True) + norm_eps)
    return centred * inverse, inverse


def normalise_back(f, normed, inverse):
    return inverse * (
        f - jnp.mean(f, -1, keepdims=True) - normed * jnp.mean(f * normed, -1, keepdims=True)
    )


gelu_a = (2.0 / jnp.pi) ** 0.5
gelu_b = 0.044715


def gelu(v):
    return 0.5 * v * (1.0 + jnp.tanh(gelu_a * (v + gelu_b * v * v * v)))


def gelu_slope(v):
    t = jnp.tanh(gelu_a * (v + gelu_b * v * v * v))
    return 0.5 * (1.0 + t) + 0.5 * v * (1.0 - t * t) * gelu_a * (1.0 + 3.0 * gelu_b * v * v)


def split_rows(x):
    return (x[:, :IMG], x[:, IMG:])


def lanes_of(hd):
    return lax.broadcasted_iota(jnp.int32, (1, 2 * hd), 1) < hd


def head_sums(x, low):
    a = jnp.sum(jnp.where(low, x, 0.0), -1, keepdims=True)
    b = jnp.sum(jnp.where(low, 0.0, x), -1, keepdims=True)
    return jnp.where(low, a, b)


def rows_of(first, second, at, width):
    return jnp.concatenate([first[0, :, pl.ds(at, width)], second[0, :, pl.ds(at, width)]], 0)


def dot_rows(a, b):
    return lax.dot_general(a, b, (((1,), (1,)), ((), ())), preferred_element_type=F32)


def dot_plain(a, b):
    return lax.dot_general(a, b, (((1,), (0,)), ((), ())), preferred_element_type=F32)


def dot_turned(a, b):
    return lax.dot_general(a, b, (((0,), (0,)), ((), ())), preferred_element_type=F32)


def pair_state(ui, ut, gains, at, model, hd, low, first_rows):
    wide = 2 * hd
    q_u, k_u, v_u = (rows_of(ui, ut, j * model + at, wide) for j in range(3))
    state = []
    for j, u in enumerate((q_u, k_u)):
        g = jnp.where(first_rows, gains[j : j + 1, :], gains[j + 2 : j + 3, :])
        r = lax.rsqrt(head_sums(u * u, low) / hd + norm_eps)
        state.append((u, g, r, (u * r * g).astype(BF)))
    return state[0], state[1], v_u.astype(BF)


def head_probs(q, k, low, bias, scale):
    scores = dot_rows(jnp.where(low, q, jnp.zeros_like(q)), k) * scale + bias
    exponent = jnp.exp(scores)
    return exponent / jnp.sum(exponent, -1, keepdims=True)


def row_kinds(image, padded, length):
    first_rows = lax.broadcasted_iota(jnp.int32, (padded, 1), 0) < image
    keys = lax.broadcasted_iota(jnp.int32, (1, padded), 1)
    return first_rows, jnp.where(keys < length, 0.0, -1e30).astype(F32)


def attention_kernel(ui, ut, gains, oi, ot, *, length, hd, pairs):
    image = ui.shape[1]
    padded = image + ut.shape[1]
    model = pairs * 2 * hd
    low = lanes_of(hd)
    first_rows, bias = row_kinds(image, padded, length)
    scale = hd**-0.5

    def one(at):
        (_, _, _, q), (_, _, _, k), v = pair_state(ui, ut, gains, at, model, hd, low, first_rows)
        both = []
        for mask in (low, jnp.logical_not(low)):
            probs = head_probs(q, k, mask, bias, scale).astype(BF)
            both.append(dot_plain(probs, v))
        out = jnp.where(low, both[0], both[1]).astype(BF)
        oi[0, :, pl.ds(at, 2 * hd)] = out[:image]
        ot[0, :, pl.ds(at, 2 * hd)] = out[image:]

    def step(i, carry):
        for j in range(2):
            one(pl.multiple_of((2 * i + j) * 2 * hd, 2 * hd))
        return carry

    lax.fori_loop(0, pairs // 2, step, 0)


def attention_back_kernel(ui, ut, gi, gt, gains, pi, pt, sums, gain_sums, *, length, hd, pairs):
    image = ui.shape[1]
    padded = image + ut.shape[1]
    wide = 2 * hd
    model = pairs * wide
    low = lanes_of(hd)
    first_rows, bias = row_kinds(image, padded, length)
    scale = hd**-0.5

    def one(at):
        (q_u, q_g, q_r, q), (k_u, k_g, k_r, k), v = pair_state(ui, ut, gains, at, model, hd, low, first_rows)
        grad = rows_of(gi, gt, at, wide)
        dqs, dks, dvs = [], [], []
        for mask in (low, jnp.logical_not(low)):
            probs = head_probs(q, k, mask, bias, scale)
            prob_grad = dot_rows(jnp.where(mask, grad, jnp.zeros_like(grad)), v)
            delta = jnp.sum(prob_grad * probs, -1, keepdims=True)
            score_grad = (probs * (prob_grad - delta)).astype(BF)
            dvs.append(dot_turned(probs.astype(BF), grad))
            dqs.append(dot_plain(score_grad, k))
            dks.append(dot_turned(score_grad, q))
        gain_rows = []
        for j, (u, g, r, pair) in enumerate(((q_u, q_g, q_r, dqs), (k_u, k_g, k_r, dks), (None, None, None, dvs))):
            t = jnp.where(low, pair[0], pair[1])
            if j < 2:
                t = t * scale
                grown = t * u * r
                gain_rows.append((jnp.sum(grown[:image], 0, keepdims=True), jnp.sum(grown[image:], 0, keepdims=True)))
                gt_ = g * t
                t = r * gt_ - u * (r * r * r) * (head_sums(u * gt_, low) / hd)
            t = t.astype(BF)
            pi[0, :, pl.ds(j * model + at, wide)] = t[:image]
            pt[0, :, pl.ds(j * model + at, wide)] = t[image:]
            wide_t = t.astype(F32)
            sums[0, 0:1, pl.ds(j * model + at, wide)] = jnp.sum(wide_t[:image], 0, keepdims=True)
            sums[0, 1:2, pl.ds(j * model + at, wide)] = jnp.sum(wide_t[image:], 0, keepdims=True)
        return jnp.concatenate([gain_rows[0][0], gain_rows[1][0], gain_rows[0][1], gain_rows[1][1]], 0)

    def step(i, total):
        for j in range(2):
            total = total + one(pl.multiple_of((2 * i + j) * wide, wide))
        return total

    gain_sums[0] = lax.fori_loop(0, pairs // 2, step, jnp.zeros((4, wide), F32))


def whole_block(x):
    return pl.BlockSpec((1,) + x.shape[1:], lambda i: (i, 0, 0))


def attention(u, gains, length):
    n, image, width = u[0].shape
    text = u[1].shape[1]
    hd = gains.shape[1] // 2
    model = width // 3
    outs = [jax.ShapeDtypeStruct((n, rows, model), BF) for rows in (image, text)]
    return pl.pallas_call(
        functools.partial(attention_kernel, length=length, hd=hd, pairs=model // (2 * hd)),
        grid=(n,),
        in_specs=[whole_block(u[0]), whole_block(u[1]), pl.BlockSpec(gains.shape, lambda i: (0, 0))],
        out_specs=[whole_block(t) for t in outs],
        out_shape=outs,
        name="attention",
    )(u[0], u[1], gains)


def attention_back(grads, u, gains, length):
    n, image, width = u[0].shape
    text = u[1].shape[1]
    hd = gains.shape[1] // 2
    model = width // 3
    outs = [jax.ShapeDtypeStruct((n, rows, width), BF) for rows in (image, text)]
    outs += [jax.ShapeDtypeStruct((n, 2, width), F32), jax.ShapeDtypeStruct((n, 4, 2 * hd), F32)]
    ins = [u[0], u[1], grads[0], grads[1]]
    pi, pt, sums, gain_sums = pl.pallas_call(
        functools.partial(attention_back_kernel, length=length, hd=hd, pairs=model // (2 * hd)),
        grid=(n,),
        in_specs=[whole_block(t) for t in ins] + [pl.BlockSpec(gains.shape, lambda i: (0, 0))],
        out_specs=[whole_block(t) for t in outs],
        out_shape=outs,
        name="attention_back",
    )(*ins, gains)
    gain = jnp.sum(gain_sums, 0)
    gain = (gain[:, :hd] + gain[:, hd:]).reshape(2, 2, hd)
    sums = jnp.sum(sums, 0)
    return [pi, pt], [sums[0], sums[1]], [gain[0], gain[1]]


def forward(x, mod, w, length):
    us, mixeds, saved = [], [], {}
    keep = {"x": x, "mod": mod}
    hidden = []
    for st in range(2):
        normed, _ = normalise(x[st].astype(F32))
        h = (normed * (1.0 + mod[:, st, 1][:, None]) + mod[:, st, 0][:, None]).astype(BF)
        h = gather_two(h)
        hidden.append(h)
        p = dot("nrd,dk->nrk", h, w["qkv"][st]) + w["b_qkv"][st]
        us.append(p)
    keep["hidden"], keep["u"] = hidden, us
    attended = attention(us, w["gain"], length)
    keep["attended"] = attended
    keep["branch"], keep["mixed"], keep["hidden_mlp"], keep["pre"], keep["act"], keep["mlp"] = [], [], [], [], [], []
    outs = []
    for st in range(2):
        branch = scatter_two(dot("nrk,kd->nrd", attended[st], w["out"][st])) + w["b_out"][st]
        mixed = x[st].astype(F32) + mod[:, st, 2][:, None] * branch
        normed, _ = normalise(mixed)
        h = (normed * (1.0 + mod[:, st, 4][:, None]) + mod[:, st, 3][:, None]).astype(BF)
        h = gather_four(h)
        pre = dot("nrd,df->nrf", h, w["fc1"][st]) + w["b_fc1"][st]
        act = gelu(pre).astype(BF)
        mlp = scatter_four(dot("nrf,fd->nrd", act, w["fc2"][st])) + w["b_fc2"][st]
        outs.append(mixed + mod[:, st, 5][:, None] * mlp)
        for name, value in (("branch", branch), ("mixed", mixed), ("hidden_mlp", h), ("pre", pre), ("act", act), ("mlp", mlp)):
            keep[name].append(value)
    return outs, keep


def backward_mlp(up, keep, w):
    mod = keep["mod"]
    state = {"mixed_grad": [], "late": [], "mlp": [], "pre": [], "fc2": [], "fc1": []}
    for st in range(2):
        mlp_grad = (mod[:, st, 5][:, None] * up[st]).astype(BF)
        state["fc2"].append(jnp.sum(mlp_grad.astype(F32), (0, 1)))
        gate = jnp.sum(keep["mlp"][st] * up[st], 1)
        mlp_grad = gather_four(mlp_grad)
        act_grad = dot("nrd,fd->nrf", mlp_grad, w["fc2"][st])
        pre_grad = (act_grad * gelu_slope(keep["pre"][st])).astype(BF)
        state["fc1"].append(jnp.sum(pre_grad.astype(F32), (0, 1)))
        h_grad = scatter_four(dot("nrf,df->nrd", pre_grad, w["fc1"][st]))
        normed, inverse = normalise(keep["mixed"][st])
        mixed_grad = up[st] + normalise_back(h_grad * (1.0 + mod[:, st, 4][:, None]), normed, inverse)
        state["late"].append((jnp.sum(h_grad, 1), jnp.sum(h_grad * normed, 1), gate))
        state["mixed_grad"].append(mixed_grad)
        state["mlp"].append(mlp_grad)
        state["pre"].append(pre_grad)
    return state


def backward_attention(state, keep, w, length):
    mod = keep["mod"]
    small = {"fc2": state["fc2"], "fc1": state["fc1"], "out": []}
    right = {"mlp": state["mlp"], "pre": state["pre"], "branch": []}
    attended_grads, gates = [], []
    for st in range(2):
        mixed_grad = state["mixed_grad"][st]
        branch_grad = (mod[:, st, 2][:, None] * mixed_grad).astype(BF)
        gates.append(jnp.sum(keep["branch"][st] * mixed_grad, 1))
        small["out"].append(jnp.sum(branch_grad.astype(F32), (0, 1)))
        branch_grad = gather_two(branch_grad)
        right["branch"].append(branch_grad)
        attended_grads.append(dot("nrd,kd->nrk", branch_grad, w["out"][st]).astype(BF))
    right["qkv"], small["qkv"], small["gain"] = attention_back(attended_grads, keep["u"], w["gain"], length)
    input_grads, mod_grads = [], []
    for st in range(2):
        h_grad = scatter_two(dot("nrk,dk->nrd", right["qkv"][st], w["qkv"][st]))
        normed, inverse = normalise(keep["x"][st].astype(F32))
        input_grads.append(
            state["mixed_grad"][st] + normalise_back(h_grad * (1.0 + mod[:, st, 1][:, None]), normed, inverse)
        )
        mod_grads.append(jnp.stack([jnp.sum(h_grad, 1), jnp.sum(h_grad * normed, 1), gates[st], *state["late"][st]], 1))
    return input_grads, jnp.stack(mod_grads, 1), small, right


def backward(up, keep, w, length):
    return backward_attention(backward_mlp(up, keep, w), keep, w, length)


def place(pieces, slots, count):
    whole = jnp.zeros((count,) + pieces[0].shape, pieces[0].dtype)
    for piece, slot in zip(pieces, slots):
        whole = lax.dynamic_update_index_in_dim(whole, piece, slot, 0)
    return whole


def take(x, index, axis):
    return lax.dynamic_index_in_dim(x, index, axis, keepdims=False)


def column_blocks(x, blocks, groups, width):
    streams, rows, _ = x.shape
    per = len(blocks) // groups

    def body(blocks_ref, x_ref, out_ref):
        out_ref[0] = x_ref[...]

    grid_spec = pltpu.PrefetchScalarGridSpec(
        num_scalar_prefetch=1,
        grid=(groups, streams, per),
        in_specs=[pl.BlockSpec((1, rows, width), lambda g, s, b, blocks: (s, 0, blocks[g * per + b]))],
        out_specs=pl.BlockSpec((1, 1, rows, width), lambda g, s, b, blocks: (g, s, 0, b)),
    )
    out = jax.ShapeDtypeStruct((groups, streams, rows, per * width), x.dtype)
    table = jnp.stack(blocks).astype(jnp.int32)
    return pl.pallas_call(body, grid_spec=grid_spec, out_shape=out, name="column_blocks")(table, x)


def columns_back(x, numbers):
    groups, streams, rows, columns = x.shape
    per = len(numbers) // groups
    width = columns // per

    def body(numbers_ref, x_ref, out_ref):
        out_ref[...] = x_ref[0].astype(F32)

    grid_spec = pltpu.PrefetchScalarGridSpec(
        num_scalar_prefetch=1,
        grid=(groups, per),
        in_specs=[pl.BlockSpec((1, streams, rows, width), lambda g, b, numbers: (g, 0, 0, b))],
        out_specs=pl.BlockSpec((streams, rows, width), lambda g, b, numbers: (0, 0, numbers[g * per + b])),
    )
    out = jax.ShapeDtypeStruct((streams, rows, groups * columns), F32)
    table = jnp.stack(numbers).astype(jnp.int32)
    return pl.pallas_call(body, grid_spec=grid_spec, out_shape=out, name="columns_back")(table, x)


def assemble(pieces, count, rows, parity):
    arrays = []
    for st in range(2):
        whole = None
        for piece, relayed, slot, at in pieces:
            if relayed is None:
                block = piece[st]
            else:
                block = jnp.where(parity == st, piece, relayed)
            if whole is None:
                whole = jnp.zeros((count * rows, block.shape[1]), block.dtype)
            whole = lax.dynamic_update_slice_in_dim(whole, block, slot * rows + at, 0)
        arrays.append(whole)
    return arrays


def prepare(w_qkv, b_qkv, gain, w_out, b_out, w_fc1, b_fc1, w_fc2, b_fc2):
    sid = lax.axis_index("shard")
    core = sid % 2
    parity = lax.axis_index("replica") % 2
    rows, width = w_qkv.shape[1], w_qkv.shape[2]
    part = width // 12
    slots = (sid, sid ^ 1, sid ^ 2, sid ^ 3)

    def of_parity(x):
        return jnp.where(parity == 0, x[0], x[1])

    numbers = [j * 4 + h * 2 + (core if g == 0 else 1 - core) for g in range(2) for j in range(3) for h in range(2)]
    mine, theirs = (t for t in column_blocks(w_qkv, numbers, 2, part))
    beside = near(theirs)
    pieces = [(mine, None, slots[0], 0), (beside, None, slots[1], 0)]
    last = None
    for block, slot in ((mine, slots[2]), (beside, slots[3])):
        chosen = of_parity(block)
        for h in range(2):
            direct = far(chosen[h * rows // 2 : (h + 1) * rows // 2])
            last = direct
            pieces.append((direct, mate(direct), slot, h * rows // 2))
    w = {"qkv": assemble(pieces, 4, rows, parity)}

    chosen = of_parity(w_out)
    chosen, last = lax.optimization_barrier((chosen, last))
    direct = far(chosen)
    relayed = mate(direct)
    half = sid // 2
    w["out"] = assemble([(w_out, None, half, 0), (direct, relayed, 1 - half, 0)], 2, rows, parity)

    columns = w_fc1.shape[2] // 4
    blocks = column_blocks(w_fc1, list(slots), 4, columns)
    beside = near(blocks[1])
    pieces = [(blocks[0], None, slots[0], 0), (beside, None, slots[1], 0)]
    for j, send in ((2, far), (3, across)):
        chosen, direct = lax.optimization_barrier((of_parity(blocks[j]), direct))
        direct = send(chosen)
        pieces.append((direct, mate(direct), slots[j], 0))
    w["fc1"] = assemble(pieces, 4, rows, parity)
    w["fc2"] = [w_fc2[0], w_fc2[1]]

    vectors = (b_qkv, b_out, b_fc2, gain.reshape(2, -1))
    packed = jnp.concatenate(vectors, 1)
    packed = gather_four(packed[None])
    packed = place([packed[j] for j in range(4)], slots, 4).astype(F32)
    flat, at = [], 0
    for vector in vectors:
        piece = packed[:, :, at : at + vector.shape[1]]
        at += vector.shape[1]
        flat.append(piece)
    b_qkv, b_out, b_fc2 = (jnp.concatenate([piece[j] for j in range(4)], 1) for piece in flat[:3])
    w["b_out"], w["b_fc2"], w["b_fc1"] = b_out, b_fc2, b_fc1.astype(F32)
    columns = [b_qkv[:, i * part : (i + 1) * part] for i in range(12)]
    w["b_qkv"] = jnp.where(core == 0, jnp.concatenate(columns[0::2], 1), jnp.concatenate(columns[1::2], 1))
    quarter = gain.shape[2]
    table = []
    for st in range(2):
        for j in range(2):
            row = [flat[3][i, st, j * quarter : (j + 1) * quarter] for i in range(4)]
            table.append(jnp.concatenate(row + row))
    w["gain"] = jnp.stack(table)
    return w


def weight_terms(left, right):
    total = None
    for a, b in zip(left, right):
        term = dot("nrd,nre->de", a, b)
        total = term if total is None else total + term
    return total


def over_replicas(x):
    return lax.psum_scatter(x, "replica", scatter_dimension=0, tiled=True)


def per_device(block_input, modulation, w_qkv, b_qkv, qk_gain, w_out, b_out, w_fc1, b_fc1, w_fc2, b_fc2, cotangent):
    section = lax.axis_index("section")
    first = section == 0
    sid = lax.axis_index("shard")
    core, row_pair = sid % 2, sid // 2
    count = lax.axis_size("replica")
    rid = lax.axis_index("replica")
    length = block_input.shape[2]
    padded = (length + 15) // 16 * 16
    w = prepare(w_qkv[0], b_qkv[0], qk_gain[0], w_out[0], b_out[0], w_fc1[0], b_fc1[0], w_fc2[0], b_fc2[0])

    def padding(x):
        return jnp.pad(x, ((0, 0), (0, 0), (0, padded - length), (0, 0)))

    def streams(x):
        return list(split_rows(x))

    def choose(a, b):
        return jax.tree.map(lambda p, q: jnp.where(first, p, q), a, b)

    def relay(x, pairs):
        return [lax.ppermute(t.astype(BF), "section", pairs) for t in x]

    block_input = padding(block_input)
    cotangent = padding(cotangent)
    mod = modulation[0]
    middle_mod = jnp.where(first, mod[1], mod[0])
    up_pair, down_pair = [(0, 1)], [(1, 0)]

    out0, keep0 = forward(streams(block_input[0]), mod[0], w, length)
    got = relay(out0, up_pair)
    out1, keep1 = forward(choose(streams(block_input[1]), got), middle_mod, w, length)
    got = relay(out1, up_pair)
    out2, keep2 = forward(got, mod[1], w, length)

    def zero_unless(cond, x):
        return [jnp.where(cond, t.astype(F32), 0.0) for t in x]

    grad0, mod_grad0, small0, right0 = backward(zero_unless(~first, streams(cotangent[0])), keep1, w, length)
    got = relay(grad0, down_pair)
    up = choose([t.astype(F32) for t in got], [t.astype(F32) for t in streams(cotangent[1])])
    keep_mid = choose(keep0, keep2)
    grad1, mod_grad1, small1, right1 = backward(up, keep_mid, w, length)
    got = relay(grad1, down_pair)
    last = backward_mlp(zero_unless(first, got), keep1, w)

    def terms(left, early, late, st):
        return weight_terms((keep_mid[left][st], keep1[left][st]), (early[st], late[st])).astype(BF)

    mlp_ends, pre_ends = choose(last["mlp"], right0["mlp"]), choose(last["pre"], right0["pre"])
    fc2 = [terms("act", right1["mlp"], mlp_ends, st) for st in (1, 0)]
    fc1 = []
    for st in (1, 0):
        t = terms("hidden_mlp", right1["pre"], pre_ends, st)
        d, cols = t.shape
        fc1.append(jnp.swapaxes(t.reshape(4, count, -1, cols), 0, 1).reshape(d, cols))
    last["mixed_grad"], fc2, fc1 = lax.optimization_barrier((last["mixed_grad"], fc2, fc1))
    fc2 = [over_replicas(t) for t in fc2]
    fc1 = [over_replicas(t) for t in fc1]
    reduced = (fc2, fc1)
    fc2 = jnp.stack([fc2[1], fc2[0]]).astype(F32)
    fc1 = [t.reshape(4, -1, t.shape[1]) for t in fc1]
    slots = [sid ^ j for j in range(4)]
    moved = []
    for j, send in ((0, lambda x: x), (1, near), (2, far), (3, across)):
        moved.append(send(jnp.stack([take(fc1[1], slots[j], 0), take(fc1[0], slots[j], 0)])))
    fc1 = columns_back(jnp.stack(moved), slots)

    grad2, mod_grad2, small2, right2 = backward_attention(last, keep1, w, length)

    def over_far(t):
        t = t.reshape(2, -1, t.shape[1])
        return (take(t, row_pair, 0).astype(F32) + far(take(t, 1 - row_pair, 0)).astype(F32)).astype(BF)

    branch_ends, qkv_ends = choose(right2["branch"], right0["branch"]), choose(right2["qkv"], right0["qkv"])
    qkv, out = [], []
    for st in (1, 0):
        t = over_far(terms("hidden", right1["qkv"], qkv_ends, st))
        cols = t.shape[1]
        qkv.append(jnp.swapaxes(t.reshape(2, count, -1, cols), 0, 1).reshape(-1, cols))
        out.append(over_far(terms("attended", right1["branch"], branch_ends, st)))
    qkv, out, _ = lax.optimization_barrier((qkv, out, reduced))
    qkv = [over_replicas(t).reshape(2, -1, t.shape[1]) for t in qkv][::-1]
    out = jnp.stack([over_replicas(t) for t in out][::-1]).astype(F32)
    own, other = (jnp.stack([take(t, which, 0) for t in qkv]) for which in (core, 1 - core))
    numbers = [j * 4 + h * 2 + c for c in (core, 1 - core) for j in range(3) for h in range(2)]
    qkv = columns_back(jnp.stack([own, near(other)]), numbers)

    small = jax.tree.map(lambda a, b, c: a + b + c, small0, small1, small2)
    pieces = []
    for st in range(2):
        cores = small["qkv"][st].reshape(6, 1, -1)
        cores = jnp.where(jnp.arange(2).reshape(1, 2, 1) == core, cores, 0.0).reshape(-1)
        quarter = small["fc1"][st].reshape(1, -1)
        quarter = jnp.where(jnp.arange(4).reshape(4, 1) == sid, quarter, 0.0).reshape(-1)
        pieces.append(jnp.concatenate([cores, small["out"][st], quarter, small["fc2"][st], small["gain"][st].reshape(-1)]))
    sizes = [w_qkv.shape[3], w_out.shape[3], w_fc1.shape[3], w_fc2.shape[3], w["gain"].shape[-1]]
    summed = lax.psum(jnp.stack(pieces), ("shard", "replica"))
    place_id = sid * count + rid
    vectors, at = [], 0
    for size in sizes:
        vectors.append(summed[:, at : at + size])
        at += size

    def own_block(x, axis):
        size = x.shape[axis] // (4 * count)
        return lax.dynamic_slice_in_dim(x, place_id * size, size, axis)

    blocks = [own_block(v, 1)[None] for v in vectors[:4]]
    gain = own_block(vectors[4].reshape(2, 2, -1), 2)[None]

    def joined(x):
        return jnp.concatenate(x, 1)[:, :length]

    activations = jnp.stack([joined(choose(out0, out1)), joined(choose(out1, out2))]).astype(BF)
    input_grads = jnp.stack([joined(choose(grad1, grad0)), joined(choose(grad2, grad1))])
    modulation_grad = jnp.stack([choose(mod_grad1, mod_grad0), choose(mod_grad2, mod_grad1)])
    return (
        activations[None],
        input_grads[None],
        modulation_grad[None],
        qkv[None],
        blocks[0],
        gain,
        out[None],
        blocks[1],
        fc1[None],
        blocks[2],
        fc2[None],
        blocks[3],
    )


def solution(mesh):
    every = ("shard", "replica")
    return jax.shard_map(
        per_device,
        mesh=mesh,
        in_specs=(
            P(None, every, None, None),
            P("section", None, every, None, None, None),
            P("section", None, "shard", None),
            P("section", None, "shard"),
            P("section", None, None, "shard"),
            P("section", None, "shard", None),
            P("section", None, "shard"),
            P("section", None, "shard", None),
            P("section", None, "shard"),
            P("section", None, "shard", None),
            P("section", None, "shard"),
            P(None, every, None, None),
        ),
        out_specs=(
            P("section", None, every, None, None),
            P("section", None, every, None, None),
            P("section", None, every, None, None, None),
            P("section", None, every, None),
            P("section", None, every),
            P("section", None, None, every),
            P("section", None, every, None),
            P("section", None, every),
            P("section", None, every, None),
            P("section", None, every),
            P("section", None, every, None),
            P("section", None, every),
        ),
        check_vma=False,
    )
```

time: 1720 us -> 1410 us (0.82)
  local copies, waits for them, and re-layouts: 464 us -> 99.9 us
  Pallas kernels: 0 us -> 114 us
  waiting for transfers between devices: 560 us -> 632 us
  other arithmetic: 217 us -> 160 us
  blocking collectives: 38.4 us -> 0 us
  matrix products: 324 us -> 297 us
    pallas_call x0 -> x10, Pallas kernels: none -> 114 us  [the longest x3 49.9 us: attention_back(): pl.pallas_call(functools.partial(attention_back_kernel, length=length, hd...]
    dynamic_update_slice x18 -> x3, local copies, waits for them, and re-layouts: 73.1 us -> 0.04 us  [place(): whole = lax.dynamic_update_index_in_dim(whole, piece, slot, 0)]
    unnamed x1164 -> x861, local copies, waits for them, and re-layouts: 102 us -> 30.8 us
    convert_element_type x16 -> x0, local copies, waits for them, and re-layouts: 49.8 us -> none  [the longest x9 19.3 us: attention_back(): whole = jnp.concatenate([back, part[2][:, :, None]], 2).astype(BF)]
    psum x1, waiting for transfers between devices: 0.01 us -> 47.3 us  [per_device(): summed = lax.psum(jnp.stack(pieces), ('shard', 'replica'))]
    reduce_sum x46 -> x32, other arithmetic: 89.7 us -> 43.3 us  [the longest x6 9.41 us: backward_mlp(): state['fc2'].append(jnp.sum(mlp_grad.astype(F32), (0, 1)))]
    slice x16 -> x2, local copies, waits for them, and re-layouts: 47.5 us -> 1.44 us  [prepare(): direct = far(chosen[h * rows // 2:(h + 1) * rows // 2])]
    reshape x7 -> x2, local copies, waits for them, and re-layouts: 45.2 us -> 4.08 us  [per_device(): t.reshape(2, count, -1, cols)]
  transfers between devices with their start and end apart: 141 -> 140, of which waited for: 45 -> 46; matrix products, arithmetic and copies ran while one was open for 51% -> 35% of each run, Pallas kernels for 0% -> 6%
where the time goes in v2:
time: 1410 us
  waiting for transfers between devices  632 us (45%)
  matrix products  297 us (21%)
  other arithmetic  160 us (11%)
  Pallas kernels  114 us (8%)
  local copies, waits for them, and re-layouts  99.9 us (7%)
  starting transfers between devices  83.7 us (6%)
  between operations  21.8 us (2%)
    dot_general x64, matrix products, dot(): return jnp.einsum(spec, a, b, preferred_element_type=F32)  297 us
    ppermute x36, waiting for transfers between devices, far(): return lax.ppermute(x, 'shard', [(i, i ^ 2) for i in range(4)])  295 us
    reduce_scatter x8, waiting for transfers between devices, over_replicas(): return lax.psum_scatter(x, 'replica', scatter_dimension=0, tiled=True)  171 us
    ppermute x7, waiting for transfers between devices, mate(): return lax.ppermute(x, 'replica', [(i, i ^ 1) for i in range(count)])  61.5 us
    pallas_call x3, Pallas kernels, attention_back(): pl.pallas_call(functools.partial(attention_back_kernel, length=length, hd...  49.9 us
    psum x1, waiting for transfers between devices, per_device(): summed = lax.psum(jnp.stack(pieces), ('shard', 'replica'))  47.3 us
    ppermute x36, starting transfers between devices, far(): return lax.ppermute(x, 'shard', [(i, i ^ 2) for i in range(4)])  37.3 us
    unnamed x861, local copies, waits for them, and re-layouts  30.8 us
  transfers between devices with their start and end apart: 140, of which 46 were waited for; matrix products, arithmetic and copies ran while one was open for 35% of the time, Pallas kernels for 6%

profile of v2, /device:TPU:0, one launch (start us, length us, event | category | flops | bytes accessed | tf_op | source)
XLA Modules:
  0.0 1408.3 jit_solution(5986469015944867761)
XLA Ops:
  13.4 16.1 %column_blocks.2 = bf16[2,2,384,2304]{3,2,1,0:T(8,128)(2,1)} custom-call(s32[12]{0:T(128)} %stack.356.blocks_ref.numbers_ref, bf16[2,384,4608]{2,1,0:T(8,128)(2,1)} %bitcast.536), custom_call_target="tpu_custom_call" | custom-call | tf_op jit(solution)/shard_map/column_blocks/pallas_call | solution.py:358
  45.5 10.4 column_blocks.3
  110.1 9.5 collective-permute-done.3
  119.6 9.5 collective-permute-done.6
  160.6 14.9 %collective-permute-done.9 = bf16[192,2304]{1,0:T(8,128)(2,1)S(1)} collective-permute-done((bf16[192,2304]{1,0:T(8,128)(2,1)S(1)}, bf16[192,2304]{1,0:T(8,128)(2,1)S(1)}, u32[]{:S(2)}, u32[]{:S(2)}) %collective-permute-start.9) | collective-permute-done | bytes 884768 | tf_op jit(solution)/shard_map/ppermute | solution.py:34
  216.4 12.2 collective-permute-done.21
  232.9 23.9 %collective-permute-done.23 = bf16[384,1536]{1,0:T(8,128)(2,1)S(1)} collective-permute-done((bf16[384,1536]{1,0:T(8,128)(2,1)S(1)}, bf16[384,1536]{1,0:T(8,128)(2,1)S(1)}, u32[]{:S(2)}, u32[]{:S(2)}) %collective-permute-start.23) | collective-permute-done | bytes 1179680 | tf_op jit(solution)/shard_map/ppermute | solution.py:29
  263.1 21.7 %collective-permute-done.24 = bf16[384,1536]{1,0:T(8,128)(2,1)S(1)} collective-permute-done((bf16[384,1536]{1,0:T(8,128)(2,1)S(1)}, bf16[384,1536]{1,0:T(8,128)(2,1)S(1)}, u32[]{:S(2)}, u32[]{:S(2)}) %collective-permute-start.24) | collective-permute-done | bytes 1179680 | tf_op jit(solution)/shard_map/ppermute | solution.py:34
  286.4 10.9 collective-permute-done.32
  461.8 11.6 collective-permute-done.52
  495.0 16.4 %attention_back.3 = (bf16[2,64,2304]{2,1,0:T(8,128)(2,1)}, bf16[2,160,2304]{2,1,0:T(8,128)(2,1)}, f32[2,2,2304]{2,1,0:T(2,128)}, f32[2,4,128]{2,1,0:T(4,128)}) custom-call(f32[2,64,2304]{2,1,0:T(8,128)} %fusion.116.ui, f32[2,160,2304]{2,1,0:T(8,128)} %fusion.85.ut, bf16[2,64,768]{2,1,0:T(8,128)(2,1)} %fusion.246.gi, bf16[2,160,768]{2,1,0:T(8,128)(2,1)} %fusion.231.gt, ...), custom_call_target="tpu_custom_call" | custom-call | tf_op jit(solution)/shard_map/attention_back/pallas_call | solution.py:237
  652.1 9.5 convert_reduce_fusion.1
  669.3 11.9 collective-permute-done.101
  694.0 11.0 fusion.185
  708.6 16.8 %attention_back.4 = (bf16[2,64,2304]{2,1,0:T(8,128)(2,1)}, bf16[2,160,2304]{2,1,0:T(8,128)(2,1)}, f32[2,2,2304]{2,1,0:T(2,128)}, f32[2,4,128]{2,1,0:T(4,128)}) custom-call(f32[2,64,2304]{2,1,0:T(8,128)} %get-tuple-element.419.ui, f32[2,160,2304]{2,1,0:T(8,128)} %get-tuple-element.421.ut, bf16[2,64,768]{2,1,0:T(8,128)(2,1)} %fusion.249.gi, ...), custom_call_target="tpu_custom_call" | custom-call | tf_op jit(solution)/shard_map/attention_back/pallas_call | solution.py:237
  806.3 9.2 fusion.5
  879.3 16.7 %attention_back.5 = (bf16[2,64,2304]{2,1,0:T(8,128)(2,1)}, bf16[2,160,2304]{2,1,0:T(8,128)(2,1)}, f32[2,2,2304]{2,1,0:T(2,128)}, f32[2,4,128]{2,1,0:T(4,128)}) custom-call(f32[2,64,2304]{2,1,0:T(8,128)} %fusion.116.ui, f32[2,160,2304]{2,1,0:T(8,128)} %fusion.85.ut, bf16[2,64,768]{2,1,0:T(8,128)(2,1)} %fusion.252.gi, bf16[2,160,768]{2,1,0:T(8,128)(2,1)} %fusion.237.gt, ...), custom_call_target="tpu_custom_call" | custom-call | tf_op jit(solution)/shard_map/attention_back/pallas_call | solution.py:237
  896.0 12.8 fusion.1
  936.0 157.6 %collective-permute-done.125 = bf16[384,1536]{1,0:T(8,128)(2,1)} collective-permute-done((bf16[384,1536]{1,0:T(8,128)(2,1)}, bf16[384,1536]{1,0:T(8,128)(2,1)}, u32[]{:S(2)}, u32[]{:S(2)}) %collective-permute-start.125) | collective-permute-done | bytes 1179680 | tf_op jit(solution)/shard_map/ppermute | solution.py:25
  1108.0 78.2 %reduce-scatter.15.cloned.1.call-done = bf16[384,1536]{1,0:T(8,128)(2,1)} async-done(((bf16[1536,1536]{1,0:T(8,128)(2,1)}), bf16[384,1536]{1,0:T(8,128)(2,1)}) %reduce-scatter.15.cloned.1.call-update) | async-done | bytes 1179664 | tf_op jit(solution)/shard_map/reduce_scatter | solution.py:470
  1209.5 47.3 %all-reduce.4.cloned.1.call-done = f32[2,13952]{1,0:T(2,128)} async-done(((f32[2,13952]{1,0:T(2,128)}), f32[2,13952]{1,0:T(2,128)}) %all-reduce.4.cloned.1.call-update) | async-done | bytes 111632 | tf_op jit(solution)/shard_map/psum | solution.py:570
  1286.2 39.7 %reduce-scatter.17.cloned.1.call-done = bf16[192,2304]{1,0:T(8,128)(2,1)} async-done(((bf16[768,2304]{1,0:T(8,128)(2,1)}), bf16[192,2304]{1,0:T(8,128)(2,1)}) %reduce-scatter.17.cloned.1.call-update) | async-done | bytes 884752 | tf_op jit(solution)/shard_map/reduce_scatter | solution.py:470
  1335.5 22.8 %reduce-scatter.23.cloned.1.call-done = bf16[96,1536]{1,0:T(8,128)(2,1)} async-done(((bf16[384,1536]{1,0:T(8,128)(2,1)}), bf16[96,1536]{1,0:T(8,128)(2,1)}) %reduce-scatter.23.cloned.1.call-update) | async-done | bytes 294928 | tf_op jit(solution)/shard_map/reduce_scatter | solution.py:470
  1358.3 30.3 %reduce-scatter.21.cloned.1.call-done = bf16[96,1536]{1,0:T(8,128)(2,1)} async-done(((bf16[384,1536]{1,0:T(8,128)(2,1)}), bf16[96,1536]{1,0:T(8,128)(2,1)}) %reduce-scatter.21.cloned.1.call-update) | async-done | bytes 294928 | tf_op jit(solution)/shard_map/reduce_scatter | solution.py:470
  (1535 shorter events, 765.8 us)
Async XLA Ops:
  8.0 1100.0 %reduce-scatter.9.cloned.1.call-start = ((), (), s32[]{:S(2)}) async-start(), calls=%async_computation.8 | async-start | bytes 5898240 | tf_op jit(solution)/shard_map/reduce_scatter | solution.py:470
  9.6 81.3 %collective-permute-start.10 = (bf16[1,2,1952]{2,1,0:T(2,128)(2,1)S(1)}, bf16[1,2,1952]{2,1,0:T(2,128)(2,1)S(1)}, u32[]{:S(2)}, u32[]{:S(2)}) collective-permute-start(bf16[1,2,1952]{2,1,0:T(2,128)(2,1)S(1)} %maximum_bitcast_fusion.4), channel_id=1, source_target_pairs={{0,4},{4,0},{8,12},{12,8},{1,5},{5,1},{9,13},{13,9},{2,6},{6,2},{1... | collective-permute-start | bytes 23432 | tf_op jit(solution)/shard_map/ppermute | solution.py:21
  10.1 80.9 %collective-permute-start.11 = (bf16[1,2,1952]{2,1,0:T(2,128)(2,1)S(1)}, bf16[1,2,1952]{2,1,0:T(2,128)(2,1)S(1)}, u32[]{:S(2)}, u32[]{:S(2)}) collective-permute-start(bf16[1,2,1952]{2,1,0:T(2,128)(2,1)S(1)} %maximum_bitcast_fusion.4), channel_id=1, source_target_pairs={{0,8},{4,12},{8,0},{12,4},{1,9},{5,13},{9,1},{13,5},{2,10},{6,14},... | collective-permute-start | bytes 23432 | tf_op jit(solution)/shard_map/ppermute | solution.py:25
  33.5 65.2 %collective-permute-start.1 = (bf16[2,384,2304]{2,1,0:T(8,128)(2,1)}, bf16[2,384,2304]{2,1,0:T(8,128)(2,1)}, u32[]{:S(2)}, u32[]{:S(2)}) collective-permute-start(bf16[2,384,2304]{2,1,0:T(8,128)(2,1)} %slice_bitcast_fusion), channel_id=1, source_target_pairs={{0,4},{4,0},{8,12},{12,8},{1,5},{5,1},{9,13},{13,9},{2,6},{6,2},{1... | collective-permute-start | bytes 10616840 | tf_op jit(solution)/shard_map/ppermute | solution.py:21
  41.4 55.4 %collective-permute-start.2 = (bf16[192,2304]{1,0:T(8,128)(2,1)}, bf16[192,2304]{1,0:T(8,128)(2,1)}, u32[]{:S(2)}, u32[]{:S(2)}) collective-permute-start(bf16[192,2304]{1,0:T(8,128)(2,1)} %get-tuple-element.312), channel_id=1, source_target_pairs={{0,8},{4,12},{8,0},{12,4},{1,9},{5,13},{9,1},{13,5},{2,10},{6,14},... | collective-permute-start | bytes 2654216 | tf_op jit(solution)/shard_map/ppermute | solution.py:25
  41.7 64.4 %collective-permute-start.4 = (bf16[192,2304]{1,0:T(8,128)(2,1)}, bf16[192,2304]{1,0:T(8,128)(2,1)}, u32[]{:S(2)}, u32[]{:S(2)}) collective-permute-start(bf16[192,2304]{1,0:T(8,128)(2,1)} %get-tuple-element.311), channel_id=1, source_target_pairs={{0,8},{4,12},{8,0},{12,4},{1,9},{5,13},{9,1},{13,5},{2,10},{6,14},... | collective-permute-start | bytes 2654216 | tf_op jit(solution)/shard_map/ppermute | solution.py:25
  95.8 289.6 %collective-permute-start.79 = (bf16[1,160,1536]{2,1,0:T(8,128)(2,1)}, bf16[1,160,1536]{2,1,0:T(8,128)(2,1)}, u32[]{:S(2)}, u32[]{:S(2)}) collective-permute-start(bf16[1,160,1536]{2,1,0:T(8,128)(2,1)} %get-tuple-element.215), channel_id=1, source_target_pairs={{0,8},{4,12},{8,0},{12,4},{1,9},{5,13},{9,1},{13,5},{2,10},{6,14},... | collective-permute-start | bytes 1474568 | tf_op jit(solution)/shard_map/ppermute | solution.py:25
  119.6 325.2 %collective-permute-start.78 = (bf16[1,160,1536]{2,1,0:T(8,128)(2,1)}, bf16[1,160,1536]{2,1,0:T(8,128)(2,1)}, u32[]{:S(2)}, u32[]{:S(2)}) collective-permute-start(bf16[1,160,1536]{2,1,0:T(8,128)(2,1)} %get-tuple-element.215), channel_id=1, source_target_pairs={{0,4},{4,0},{8,12},{12,8},{1,5},{5,1},{9,13},{13,9},{2,6},{6,2},{1... | collective-permute-start | bytes 1474568 | tf_op jit(solution)/shard_map/ppermute | solution.py:21
  385.8 59.0 %collective-permute-start.80 = (bf16[1,160,1536]{2,1,0:T(8,128)(2,1)}, bf16[1,160,1536]{2,1,0:T(8,128)(2,1)S(1)}, u32[]{:S(2)}, u32[]{:S(2)}) collective-permute-start(bf16[1,160,1536]{2,1,0:T(8,128)(2,1)} %collective-permute-done.79), channel_id=1, source_target_pairs={{0,4},{4,0},{8,12},{12,8},{1,5},{5,1},{9,13},{13,9},{2,6},{6,2},{1... | collective-permute-start | bytes 1474568 | tf_op jit(solution)/shard_map/ppermute | solution.py:21
  540.7 65.4 %collective-permute-start.87 = (bf16[1,64,1536]{2,1,0:T(8,128)(2,1)}, bf16[1,64,1536]{2,1,0:T(8,128)(2,1)}, u32[]{:S(2)}, u32[]{:S(2)}) collective-permute-start(bf16[1,64,1536]{2,1,0:T(8,128)(2,1)} %get-tuple-element.199), channel_id=1, source_target_pairs={{0,4},{4,0},{8,12},{12,8},{1,5},{5,1},{9,13},{13,9},{2,6},{6,2},{1... | collective-permute-start | bytes 589832 | tf_op jit(solution)/shard_map/ppermute | solution.py:21
  835.0 273.0 %reduce-scatter.11.cloned.1.call-start = ((), (), s32[]{:S(2)}) async-start(), calls=%async_computation.9 | async-start | bytes 5898240 | tf_op jit(solution)/shard_map/reduce_scatter | solution.py:470
  835.8 272.2 %reduce-scatter.13.cloned.1.call-start = ((), (), s32[]{:S(2)}) async-start(), calls=%async_computation.10 | async-start | bytes 5898240 | tf_op jit(solution)/shard_map/reduce_scatter | solution.py:470
  836.5 349.6 %reduce-scatter.15.cloned.1.call-start = ((), (), s32[]{:S(2)}) async-start(), calls=%async_computation.11 | async-start | bytes 5898240 | tf_op jit(solution)/shard_map/reduce_scatter | solution.py:470
  861.6 395.2 %all-reduce.4.cloned.1.call-start = ((), (), s32[]{:S(2)}) async-start(), calls=%async_computation.14 | async-start | bytes 223232 | tf_op jit(solution)/shard_map/psum | solution.py:570
  871.7 61.6 %collective-permute-start.126 = (bf16[384,1536]{1,0:T(8,128)(2,1)}, bf16[384,1536]{1,0:T(8,128)(2,1)}, u32[]{:S(2)}, u32[]{:S(2)}) collective-permute-start(bf16[384,1536]{1,0:T(8,128)(2,1)} %dynamic-slice_bitcast_fusion.2), channel_id=1, source_target_pairs={{0,8},{4,12},{8,0},{12,4},{1,9},{5,13},{9,1},{13,5},{2,10},{6,14},... | collective-permute-start | bytes 3538952 | tf_op jit(solution)/shard_map/ppermute | solution.py:25
  912.9 183.7 %collective-permute-start.123 = (bf16[768,2304]{1,0:T(8,128)(2,1)}, bf16[768,2304]{1,0:T(8,128)(2,1)}, u32[]{:S(2)}, u32[]{:S(2)}) collective-permute-start(bf16[768,2304]{1,0:T(8,128)(2,1)} %dynamic-slice_bitcast_fusion.1), channel_id=1, source_target_pairs={{0,8},{4,12},{8,0},{12,4},{1,9},{5,13},{9,1},{13,5},{2,10},{6,14},... | collective-permute-start | bytes 10616840 | tf_op jit(solution)/shard_map/ppermute | solution.py:25
  923.1 177.8 %collective-permute-start.124 = (bf16[768,2304]{1,0:T(8,128)(2,1)}, bf16[768,2304]{1,0:T(8,128)(2,1)}, u32[]{:S(2)}, u32[]{:S(2)}) collective-permute-start(bf16[768,2304]{1,0:T(8,128)(2,1)} %dynamic-slice_bitcast_fusion), channel_id=1, source_target_pairs={{0,8},{4,12},{8,0},{12,4},{1,9},{5,13},{9,1},{13,5},{2,10},{6,14},... | collective-permute-start | bytes 10616840 | tf_op jit(solution)/shard_map/ppermute | solution.py:25
  930.5 163.1 %collective-permute-start.125 = (bf16[384,1536]{1,0:T(8,128)(2,1)}, bf16[384,1536]{1,0:T(8,128)(2,1)}, u32[]{:S(2)}, u32[]{:S(2)}) collective-permute-start(bf16[384,1536]{1,0:T(8,128)(2,1)} %dynamic-slice_bitcast_fusion.3), channel_id=1, source_target_pairs={{0,8},{4,12},{8,0},{12,4},{1,9},{5,13},{9,1},{13,5},{2,10},{6,14},... | collective-permute-start | bytes 3538952 | tf_op jit(solution)/shard_map/ppermute | solution.py:25
  933.1 351.9 %reduce-scatter.19.cloned.1.call-start = ((), (), s32[]{:S(2)}) async-start(), calls=%async_computation.13 | async-start | bytes 4423680 | tf_op jit(solution)/shard_map/reduce_scatter | solution.py:470
  1186.3 139.6 %reduce-scatter.17.cloned.1.call-start = ((), (), s32[]{:S(2)}) async-start(), calls=%async_computation.12 | async-start | bytes 4423680 | tf_op jit(solution)/shard_map/reduce_scatter | solution.py:470
  1196.0 162.3 %reduce-scatter.23.cloned.1.call-start = ((), (), s32[]{:S(2)}) async-start(), calls=%async_computation.16 | async-start | bytes 1474560 | tf_op jit(solution)/shard_map/reduce_scatter | solution.py:470
  1203.4 61.9 %collective-permute-start.122 = (bf16[1,160,1536]{2,1,0:T(8,128)(2,1)}, bf16[1,160,1536]{2,1,0:T(8,128)(2,1)S(1)}, u32[]{:S(2)}, u32[]{:S(2)}) collective-permute-start(bf16[1,160,1536]{2,1,0:T(8,128)(2,1)} %slice.1752), channel_id=1, source_target_pairs={{0,4},{4,0},{8,12},{12,8},{1,5},{5,1},{9,13},{13,9},{2,6},{6,2},{1... | collective-permute-start | bytes 1474568 | tf_op jit(solution)/shard_map/ppermute | solution.py:21
  1269.5 119.1 %reduce-scatter.21.cloned.1.call-start = ((), (), s32[]{:S(2)}) async-start(), calls=%async_computation.15 | async-start | bytes 1474560 | tf_op jit(solution)/shard_map/reduce_scatter | solution.py:470
  1327.2 63.6 %collective-permute-start.127 = (bf16[2,96,2304]{2,1,0:T(8,128)(2,1)S(1)}, bf16[2,96,2304]{2,1,0:T(8,128)(2,1)S(1)}, u32[]{:S(2)}, u32[]{:S(2)}) collective-permute-start(bf16[2,96,2304]{2,1,0:T(8,128)(2,1)S(1)} %pad_maximum_fusion.17), channel_id=1, source_target_pairs={{0,4},{4,0},{8,12},{12,8},{1,5},{5,1},{9,13},{13,9},{2,6},{6,2},{1... | collective-permute-start | bytes 2654216 | tf_op jit(solution)/shard_map/ppermute | solution.py:21
  (524 other events, 9154.4 us)
Sparse Core Ops, SparseCore 0:
  835.1 85.7 reduce-scatter.8
  923.2 86.1 reduce-scatter.10
  1011.8 85.9 reduce-scatter.12
  1100.0 86.1 reduce-scatter.14
  1188.9 67.3 reduce-scatter.18
  1259.0 66.8 reduce-scatter.16
  1328.8 29.4 reduce-scatter.22
  1360.6 27.9 reduce-scatter.20
Sparse Core Ops, SparseCore 1:
  933.2 323.6 all-reduce.3
